TPU v7x, 32 devices: a whole 2x2x4 slice. The times are simulated.
32 devices in a mesh: dp: 2 (over y), row: 4 (over x, core), col: 4 (over z).
Axes of the slice: x: 2, y: 2, z: 4, core: 2. Of those that a mesh axis runs over, the one named last changes fastest.
Arguments:
- hidden_in: bfloat16 [8192, 1024], P(('dp', 'col'), 'row'), may hold values from -6 to 6
- norm_gain: bfloat16 [1024], P('row'), may hold values from 0.5 to 1.5
- w_qkv: bfloat16 [1024, 8, 256], P('row', 'col'), may hold values from -0.1875 to 0.1875
- w_out: bfloat16 [8, 128, 1024], P('col', None, 'row'), may hold values from -1.5 to 1.5
- ffn_gain: bfloat16 [1024], P('row'), may hold values from 0.5 to 1.5
- router: bfloat16 [1024, 32], P('row'), may hold values from -0.09375 to 0.09375
- w_gate: bfloat16 [32, 1024, 512], P(('dp', 'row')), may hold values from -0.1875 to 0.1875
- w_up: bfloat16 [32, 1024, 512], P(('dp', 'row')), may hold values from -0.1875 to 0.1875
- w_down: bfloat16 [32, 512, 1024], P(('dp', 'row')), may hold values from -1 to 1
- cotangent: bfloat16 [8192, 1024], P(('dp', 'col'), 'row'), may hold values from -6 to 6
- segment_ids: int32 [8, 1024], P(('dp', 'row')), may hold values from 0 to 3, never falling along the last dimension, each value on 1 to 512 neighbouring positions
- expert_ids: int32 [8192, 8], P(('dp', 'col')), may hold values from 0 to 31, all different within a row
- pair_order: int32 [8192, 8], P(('dp', 'col')), may hold values from 0 to 8191, as said below
Outputs:
- layer_out: bfloat16 [8192, 1024], P(('dp', 'col'), 'row')
- grad_in: float32 [8192, 1024], P(('dp', 'col'), 'row')
- grad_norm_gain: float32 [1024], P('row')
- grad_qkv: float32 [1024, 8, 256], P('row', 'col')
- grad_out: float32 [8, 128, 1024], P('col', None, 'row')
- grad_ffn_gain: float32 [1024], P('row')
- grad_router: float32 [1024, 32], P('row')
- grad_gate: float32 [32, 1024, 512], P(('dp', 'row'))
- grad_up: float32 [32, 1024, 512], P(('dp', 'row'))
- grad_down: float32 [32, 512, 1024], P(('dp', 'row'))
Inputs may be any that keep to these rules, and one draw needn't show every extreme that they name: Within each block of 1024 consecutive tokens, read row by row, pair_order holds every number of 0 to 8191 once.
All inputs are finite; a program needn't handle non-finite values.
Results may differ from a plain program's by a relative error of at most 0.024.
Values may be sent and summed in bfloat16 or wider, within the bound.
A program may use at most 192 MiB of HBM per device.

v0:
```python
import jax
import jax.numpy as jnp
from jax import lax
from jax.sharding import PartitionSpec as P

D = 1024
HQ = 16
HK = 8
HD = 64
EXPERTS = 32
TOP = 8


EPSILON = 1e-06
ROPE_BASE = 10000.0
NEG_LARGE = -1e30
HIGHEST = lax.Precision.HIGHEST


def rotate(values, cosine, sine_table):
    half_size = values.shape[-1] // 2
    lower_half = values[..., :half_size]
    upper_half = values[..., half_size:]
    return jnp.concatenate(
        [
            lower_half * cosine - upper_half * sine_table,
            upper_half * cosine + lower_half * sine_table,
        ],
        axis=-1,
    )


def rotate_back(values, cosine, sine_table):
    half_size = values.shape[-1] // 2
    lower_half = values[..., :half_size]
    upper_half = values[..., half_size:]
    return jnp.concatenate(
        [
            lower_half * cosine + upper_half * sine_table,
            upper_half * cosine - lower_half * sine_table,
        ],
        axis=-1,
    )


def rope_tables(length, head_size):
    positions = jnp.arange(length, dtype=jnp.float32)
    frequency = ROPE_BASE ** (-2.0 * jnp.arange(head_size // 2, dtype=jnp.float32) / head_size)
    angles = positions[:, None] * frequency[None, :]
    return (jnp.cos(angles), jnp.sin(angles))


def visible(segment_row):
    positions = jnp.arange(segment_row.shape[-1], dtype=jnp.int32)
    causal = positions[:, None] >= positions[None, :]
    return causal & (segment_row[..., :, None] == segment_row[..., None, :])


def pair_ranks(expert_ids, pair_order, block_rows):
    experts_flat = expert_ids.reshape(-1, block_rows * TOP)
    order_flat = pair_order.reshape(-1, block_rows * TOP)

    def one_block(experts_row, order_row):
        pair_count = experts_row.shape[0]
        by_order = (
            jnp.zeros((pair_count,), jnp.int32)
            .at[order_row]
            .set(jnp.arange(pair_count, dtype=jnp.int32))
        )
        sorted_experts = experts_row[by_order]
        onehot = (sorted_experts[:, None] == jnp.arange(EXPERTS, dtype=jnp.int32)[None, :]).astype(
            jnp.int32
        )
        before = jnp.cumsum(onehot, axis=0) - onehot
        sorted_rank = jnp.sum(before * onehot, axis=1)
        return sorted_rank[order_row]

    return jax.vmap(one_block)(experts_flat, order_flat).reshape(expert_ids.shape)


def feature_total(values):
    return lax.psum(values, "row")


def tokens_by_col(values):
    return lax.all_gather(values, "col", axis=0, tiled=True)


def tokens_by_row(values):
    return lax.all_gather(values, "row", axis=0, tiled=True)


def col_scatter(term_fn, keep_rows):
    return lax.psum_scatter(
        term_fn(jnp.int32(0), keep_rows * lax.axis_size("col")),
        "col",
        scatter_dimension=0,
        tiled=True,
    )


def to_experts(outgoing):
    arrived = lax.all_to_all(outgoing, ("dp", "row"), split_axis=0, concat_axis=0, tiled=True)
    return arrived


def from_experts(outgoing):
    arrived = lax.all_to_all(outgoing, ("dp", "row"), split_axis=0, concat_axis=0, tiled=True)
    return arrived


def owner_layout(incoming, dp_count, row_count, exp_local):
    capacity = incoming.shape[1] // exp_local
    part_width = incoming.shape[2]
    sectioned = incoming.reshape(dp_count, row_count, exp_local, capacity, part_width)
    return sectioned.transpose(2, 0, 3, 1, 4).reshape(
        exp_local, dp_count * capacity, row_count * part_width
    )


def source_layout(owner_rows, dp_count, row_count):
    exp_local, slot_rows, full_width = owner_rows.shape
    capacity = slot_rows // dp_count
    part_width = full_width // row_count
    sectioned = owner_rows.reshape(exp_local, dp_count, capacity, row_count, part_width)
    return sectioned.transpose(1, 3, 0, 2, 4).reshape(
        dp_count * row_count, exp_local * capacity, part_width
    )


def attend_forward(pack):
    query_seq, key_seq, value_seq, segment_seq = pack
    score_scale = query_seq.shape[-1] ** (-0.5)
    scores = (
        jnp.einsum("qhgd,khd->hgqk", query_seq, key_seq, preferred_element_type=jnp.float32)
        * score_scale
    )
    scores = jnp.where(visible(segment_seq), scores, NEG_LARGE)
    row_max = jnp.max(scores, axis=-1, keepdims=True)
    weights = jnp.exp(scores - row_max)
    row_total = jnp.sum(weights, axis=-1, keepdims=True)
    weights_low = (weights / row_total).astype(jnp.bfloat16)
    mixed_seq = jnp.einsum(
        "hgqk,khd->qhgd", weights_low, value_seq, preferred_element_type=jnp.float32
    )
    return (mixed_seq.astype(jnp.bfloat16), row_max + jnp.log(row_total))


def attend_backward(pack):
    query_seq, key_seq, value_seq, segment_seq, log_total, grad_seq = pack
    score_scale = query_seq.shape[-1] ** (-0.5)
    scores = (
        jnp.einsum("qhgd,khd->hgqk", query_seq, key_seq, preferred_element_type=jnp.float32)
        * score_scale
    )
    scores = jnp.where(visible(segment_seq), scores, NEG_LARGE)
    weights = jnp.exp(scores - log_total)
    grad_weights = jnp.einsum(
        "qhgd,khd->hgqk", grad_seq, value_seq, preferred_element_type=jnp.float32
    )
    inner_sum = jnp.sum(weights * grad_weights, axis=-1, keepdims=True)
    grad_scores = (weights * (grad_weights - inner_sum)).astype(jnp.bfloat16)
    grad_values = jnp.einsum(
        "hgqk,qhgd->khd", weights.astype(jnp.bfloat16), grad_seq, preferred_element_type=jnp.float32
    )
    grad_query = (
        jnp.einsum("hgqk,khd->qhgd", grad_scores, key_seq, preferred_element_type=jnp.float32)
        * score_scale
    )
    grad_key = (
        jnp.einsum("hgqk,qhgd->khd", grad_scores, query_seq, preferred_element_type=jnp.float32)
        * score_scale
    )
    return (grad_query, grad_key, grad_values)


def on_device(
    hidden_in,
    norm_gain,
    w_qkv,
    w_out,
    ffn_gain,
    router,
    w_gate,
    w_up,
    w_down,
    cotangent,
    segment_ids,
    expert_ids,
    pair_order,
):
    dp_count = lax.axis_size("dp")
    row_count = lax.axis_size("row")
    owners = dp_count * row_count
    tok_rows, part_width = hidden_in.shape
    seq_count, length = segment_ids.shape
    att_rows = seq_count * length
    kv_local = w_qkv.shape[1]
    group_size = HQ // HK
    exp_local = w_gate.shape[0]
    capacity = tok_rows * TOP // EXPERTS
    total_slots = EXPERTS * capacity
    resid_in = hidden_in.astype(jnp.float32)
    gain_one = norm_gain.astype(jnp.float32)
    rstd_one = lax.rsqrt(feature_total(jnp.sum(resid_in * resid_in, axis=1)) / D + EPSILON)
    normed_one = (resid_in * rstd_one[:, None] * gain_one).astype(jnp.bfloat16)
    group_rows = tokens_by_col(normed_one)
    qkv_flat = w_qkv.reshape(part_width, -1)
    picked = group_rows
    qkv_local = lax.psum_scatter(
        jnp.dot(picked, qkv_flat, preferred_element_type=jnp.float32),
        "row",
        scatter_dimension=0,
        tiled=True,
    )
    qkv_local = qkv_local.reshape(seq_count, length, kv_local, -1)
    cosine, sine_table = rope_tables(length, HD)
    queries = qkv_local[..., : group_size * HD].reshape(seq_count, length, kv_local, group_size, HD)
    query_rot = rotate(
        queries, cosine[None, :, None, None, :], sine_table[None, :, None, None, :]
    ).astype(jnp.bfloat16)
    key_rot = rotate(
        qkv_local[..., group_size * HD : (group_size + 1) * HD],
        cosine[None, :, None, :],
        sine_table[None, :, None, :],
    ).astype(jnp.bfloat16)
    value_low = qkv_local[..., (group_size + 1) * HD :].astype(jnp.bfloat16)
    mixed_heads, log_total = lax.map(attend_forward, (query_rot, key_rot, value_low, segment_ids))
    mixed_rows = tokens_by_row(mixed_heads.reshape(att_rows, -1))
    out_flat = w_out.reshape(-1, part_width)

    def out_term(first_row, block_rows):
        return jnp.dot(mixed_rows, out_flat, preferred_element_type=jnp.float32)

    resid_mid = resid_in + col_scatter(out_term, tok_rows)
    gain_two = ffn_gain.astype(jnp.float32)
    router_float = router.astype(jnp.float32)
    square_two, logit_part = (
        lax.psum(jnp.sum(resid_mid * resid_mid, axis=1).astype(jnp.bfloat16), "row").astype(
            jnp.float32
        ),
        lax.psum(
            jnp.dot(resid_mid * gain_two, router_float, precision=HIGHEST).astype(jnp.bfloat16),
            "row",
        ).astype(jnp.float32),
    )
    rstd_two = lax.rsqrt(square_two / D + EPSILON)
    logits = logit_part * rstd_two[:, None]
    normed_float = resid_mid * rstd_two[:, None] * gain_two
    normed_two = normed_float.astype(jnp.bfloat16)
    choose = (expert_ids[:, :, None] == jnp.arange(EXPERTS, dtype=jnp.int32)[None, None, :]).astype(
        jnp.float32
    )
    gate_weights = jax.nn.softmax(jnp.sum(choose * logits[:, None, :], axis=2), axis=1)
    pair_rank = pair_ranks(expert_ids, pair_order, tok_rows)
    pair_slot = jnp.where(pair_rank < capacity, expert_ids * capacity + pair_rank, total_slots)
    pair_index = jnp.arange(tok_rows * TOP, dtype=jnp.int32)
    slot_pair = (
        jnp.full((total_slots + 1,), tok_rows * TOP, jnp.int32)
        .at[pair_slot.reshape(-1)]
        .set(pair_index)[:total_slots]
    )
    padded_two = jnp.concatenate([normed_two, jnp.zeros((1, part_width), jnp.bfloat16)], axis=0)
    outgoing = padded_two[slot_pair // TOP].reshape(owners, exp_local * capacity, part_width)
    expert_rows = owner_layout(to_experts(outgoing), dp_count, row_count, exp_local)
    gate_pre = jnp.einsum("erd,edf->erf", expert_rows, w_gate, preferred_element_type=jnp.float32)
    up_pre = jnp.einsum("erd,edf->erf", expert_rows, w_up, preferred_element_type=jnp.float32)
    hidden = (jax.nn.silu(gate_pre) * up_pre).astype(jnp.bfloat16)
    expert_out = jnp.einsum(
        "erf,efd->erd", hidden, w_down, preferred_element_type=jnp.float32
    ).astype(jnp.bfloat16)
    returned = from_experts(source_layout(expert_out, dp_count, row_count))
    slot_table = jnp.concatenate(
        [returned.reshape(total_slots, part_width), jnp.zeros((1, part_width), jnp.bfloat16)],
        axis=0,
    )
    pair_rows = slot_table[pair_slot].astype(jnp.float32)
    layer_sum = resid_mid + jnp.einsum("tk,tkd->td", gate_weights, pair_rows, precision=HIGHEST)
    grad_top = cotangent.astype(jnp.float32)
    grad_gates = lax.psum(jnp.einsum("td,tkd->tk", grad_top, pair_rows, precision=HIGHEST), "row")
    pair_grad = (gate_weights[:, :, None] * grad_top[:, None, :]).astype(jnp.bfloat16)
    grad_padded = jnp.concatenate(
        [pair_grad.reshape(tok_rows * TOP, part_width), jnp.zeros((1, part_width), jnp.bfloat16)],
        axis=0,
    )
    outgoing_grad = grad_padded[slot_pair].reshape(owners, exp_local * capacity, part_width)
    grad_rows = owner_layout(to_experts(outgoing_grad), dp_count, row_count, exp_local)
    grad_hidden = jnp.einsum("erd,efd->erf", grad_rows, w_down, preferred_element_type=jnp.float32)
    sigmoid_gate = jax.nn.sigmoid(gate_pre)
    grad_gate_pre = (
        grad_hidden * up_pre * sigmoid_gate * (1.0 + gate_pre * (1.0 - sigmoid_gate))
    ).astype(jnp.bfloat16)
    grad_up_pre = (grad_hidden * gate_pre * sigmoid_gate).astype(jnp.bfloat16)
    grad_down_local = jnp.einsum(
        "erf,erd->efd", hidden, grad_rows, preferred_element_type=jnp.float32
    )
    grad_gate_local = jnp.einsum(
        "erd,erf->edf", expert_rows, grad_gate_pre, preferred_element_type=jnp.float32
    )
    grad_up_local = jnp.einsum(
        "erd,erf->edf", expert_rows, grad_up_pre, preferred_element_type=jnp.float32
    )
    rows_back = jnp.einsum(
        "erf,edf->erd", grad_gate_pre, w_gate, preferred_element_type=jnp.float32
    )
    rows_back = (
        rows_back
        + jnp.einsum("erf,edf->erd", grad_up_pre, w_up, preferred_element_type=jnp.float32)
    ).astype(jnp.bfloat16)
    returned_grad = from_experts(source_layout(rows_back, dp_count, row_count))
    grad_table = jnp.concatenate(
        [returned_grad.reshape(total_slots, part_width), jnp.zeros((1, part_width), jnp.bfloat16)],
        axis=0,
    )
    inner_gate = jnp.sum(gate_weights * grad_gates, axis=1, keepdims=True)
    grad_chosen = gate_weights * (grad_gates - inner_gate)
    grad_logits = jnp.einsum("tk,tke->te", grad_chosen, choose, precision=HIGHEST)
    grad_router_part = jnp.einsum("td,te->de", normed_float, grad_logits, precision=HIGHEST)
    grad_normed = jnp.sum(grad_table[pair_slot].astype(jnp.float32), axis=1)
    grad_normed = grad_normed + jnp.einsum(
        "te,de->td", grad_logits, router_float, precision=HIGHEST
    )
    grad_gain_two_part = jnp.sum(grad_normed * resid_mid * rstd_two[:, None], axis=0)
    scaled_two = grad_normed * gain_two
    inner_two = feature_total(jnp.sum(scaled_two * resid_mid, axis=1))
    grad_resid = (
        grad_top
        + rstd_two[:, None] * scaled_two
        - resid_mid * (rstd_two * rstd_two * rstd_two * inner_two / D)[:, None]
    )
    branch_rows = tokens_by_col(grad_resid.astype(jnp.bfloat16))
    grad_out_local = jnp.einsum(
        "tc,td->cd", mixed_rows, branch_rows, preferred_element_type=jnp.float32
    ).reshape(w_out.shape)
    picked = branch_rows
    grad_mixed = lax.psum_scatter(
        jnp.einsum("td,cd->tc", picked, out_flat, preferred_element_type=jnp.float32).astype(
            jnp.bfloat16
        ),
        "row",
        scatter_dimension=0,
        tiled=True,
    ).astype(jnp.float32)
    grad_mixed = grad_mixed.astype(jnp.bfloat16).reshape(
        seq_count, length, kv_local, group_size, HD
    )
    grad_query, grad_key, grad_values = lax.map(
        attend_backward, (query_rot, key_rot, value_low, segment_ids, log_total, grad_mixed)
    )
    grad_query = rotate_back(
        grad_query, cosine[None, :, None, None, :], sine_table[None, :, None, None, :]
    )
    grad_key = rotate_back(grad_key, cosine[None, :, None, :], sine_table[None, :, None, :])
    grad_qkv_pre = jnp.concatenate(
        [grad_query.reshape(seq_count, length, kv_local, group_size * HD), grad_key, grad_values],
        axis=-1,
    )
    grad_qkv_pre = grad_qkv_pre.astype(jnp.bfloat16).reshape(att_rows, -1)
    qkv_rows = tokens_by_row(grad_qkv_pre)
    grad_qkv_local = jnp.einsum(
        "td,tc->dc", group_rows, qkv_rows, preferred_element_type=jnp.float32
    ).reshape(w_qkv.shape)

    def normed_term(first_row, block_rows):
        return jnp.einsum("tc,dc->td", qkv_rows, qkv_flat, preferred_element_type=jnp.float32)

    grad_normed_one = col_scatter(normed_term, tok_rows)
    grad_gain_one_part = jnp.sum(grad_normed_one * resid_in * rstd_one[:, None], axis=0)
    scaled_one = grad_normed_one * gain_one
    inner_one = feature_total(jnp.sum(scaled_one * resid_in, axis=1))
    grad_in = (
        grad_resid
        + rstd_one[:, None] * scaled_one
        - resid_in * (rstd_one * rstd_one * rstd_one * inner_one / D)[:, None]
    )
    col_sums = (
        lax.psum(grad_gate_local.astype(jnp.bfloat16), "col").astype(jnp.float32),
        lax.psum(grad_up_local.astype(jnp.bfloat16), "col").astype(jnp.float32),
        lax.psum(grad_down_local.astype(jnp.bfloat16), "col").astype(jnp.float32),
        lax.psum(grad_router_part.astype(jnp.bfloat16), "col").astype(jnp.float32),
        lax.psum(grad_gain_one_part.astype(jnp.bfloat16), "col").astype(jnp.float32),
        lax.psum(grad_gain_two_part.astype(jnp.bfloat16), "col").astype(jnp.float32),
    )
    dp_sums = (
        lax.psum(grad_qkv_local.astype(jnp.bfloat16), "dp").astype(jnp.float32),
        lax.psum(grad_out_local.astype(jnp.bfloat16), "dp").astype(jnp.float32),
        lax.psum(col_sums[3].astype(jnp.bfloat16), "dp").astype(jnp.float32),
        lax.psum(col_sums[4].astype(jnp.bfloat16), "dp").astype(jnp.float32),
        lax.psum(col_sums[5].astype(jnp.bfloat16), "dp").astype(jnp.float32),
    )
    return (
        layer_sum.astype(jnp.bfloat16),
        grad_in,
        dp_sums[3],
        dp_sums[0],
        dp_sums[1],
        dp_sums[4],
        dp_sums[2],
        col_sums[0],
        col_sums[1],
        col_sums[2],
    )


def solution(mesh):
    placed = (
        P(("dp", "col"), "row"),
        P("row"),
        P("row", "col", None),
        P("col", None, "row"),
        P("row"),
        P("row", None),
        P(("dp", "row"), None, None),
        P(("dp", "row"), None, None),
        P(("dp", "row"), None, None),
        P(("dp", "col"), "row"),
        P(("dp", "row"), None),
        P(("dp", "col"), None),
        P(("dp", "col"), None),
    )
    return jax.shard_map(
        on_device,
        mesh=mesh,
        in_specs=placed,
        out_specs=(
            P(("dp", "col"), "row"),
            P(("dp", "col"), "row"),
            P("row"),
            P("row", "col", None),
            P("col", None, "row"),
            P("row"),
            P("row", None),
            P(("dp", "row"), None, None),
            P(("dp", "row"), None, None),
            P(("dp", "row"), None, None),
        ),
        check_vma=False,
    )
```

profile of v0, /device:TPU:2, one launch (start us, length us, event | category | flops | bytes accessed | tf_op | source)
XLA Modules:
  0.0 1592.3 jit_solution(2204811040730047514)
XLA Ops:
  18.7 46.5 %all-gather.5.cloned.1.call-done = bf16[4096,256]{1,0:T(8,128)(2,1)} async-done(((bf16[1024,256]{1,0:T(8,128)(2,1)}), bf16[4096,256]{1,0:T(8,128)(2,1)}) %all-gather.5.cloned.1.call-update) | async-done | bytes 2097168 | tf_op jit(solution)/shard_map/all_gather | solution.py:86
  73.7 67.2 %reduce-scatter.5.cloned.1.call-done = f32[1024,512]{1,0:T(8,128)} async-done(((f32[4096,512]{1,0:T(8,128)}), f32[1024,512]{1,0:T(8,128)}) %reduce-scatter.5.cloned.1.call-update) | async-done | bytes 2097168 | tf_op jit(solution)/shard_map/reduce_scatter | solution.py:210
  179.1 30.5 %scatter_custom_fusion.1 = s32[8192]{0:T(1024)S(1)} fusion(s32[8192]{0:T(1024)S(1)} %broadcast_select_fusion, s32[8192]{0:T(1024)S(1)} %iota.84, s32[]{:T(128)} %constant.106.clone.1), kind=kCustom, calls=%fused_computation.158 | custom fusion | bytes 32772
  216.4 48.0 %gather_fusion.4 = s32[8192]{0:T(1024)S(1)} fusion(s32[1,8192]{1,0:T(1,128)S(1)} %reshape.461, s32[8192]{0:T(1024)S(1)} %bitcast.176), kind=kCustom, calls=%fused_computation.4 | custom fusion | bytes 131072 | tf_op jit(solution)/shard_map/vmap()/gather | solution.py:70
  276.5 48.0 %gather_fusion.5 = s32[8192]{0:T(1024)S(1)} fusion(s32[1,8192]{1,0:T(1,128)S(1)} %bitcast.175, s32[8192]{0:T(1024)S(1)} %bitcast.177), kind=kCustom, calls=%fused_computation.5 | custom fusion | bytes 131072 | tf_op jit(solution)/shard_map/vmap()/gather | solution.py:76
  325.2 30.5 %scatter_custom_fusion = s32[8193]{0:T(1024)S(1)} fusion(s32[8192]{0:T(1024)S(1)} %bitcast.202, s32[8192]{0:T(1024)S(1)} %iota.80, s32[]{:T(128)} %constant.105.clone.1), kind=kCustom, calls=%fused_computation.152 | custom fusion | bytes 32776 | tf_op jit(solution)/shard_map/scatter | solution.py:261
  364.6 33.2 %gather_fusion = bf16[8192,256]{1,0:T(8,128)(2,1)} fusion(bf16[1025,256]{1,0:T(8,128)(2,1)S(1)} %concatenate.54, s32[8192]{0:T(1024)S(1)} %get-tuple-element.97), kind=kCustom, calls=%fused_computation | custom fusion | bytes 8421376 | tf_op jit(solution)/shard_map/gather | solution.py:264
  397.8 52.0 %all_to_all.20 = bf16[8,1024,256]{2,1,0:T(8,128)(2,1)S(1)} all-to-all(bf16[8,1024,256]{2,1,0:T(8,128)(2,1)} %bitcast.184), channel_id=1, replica_groups=mesh['dp'=2,'row'=4,'col'=4] {'dp','row'}, dimensions={0} | all-to-all | bytes 8388608 | tf_op jit(solution)/shard_map/all_to_all | solution.py:103
  499.7 33.2 %all-reduce.12.cloned.1.call-done = bf16[1024,32]{0,1:T(8,128)(2,1)} async-done(((bf16[1024,32]{0,1:T(8,128)(2,1)}), bf16[1024,32]{0,1:T(8,128)(2,1)}) %all-reduce.12.cloned.1.call-update) | async-done | bytes 65552 | tf_op jit(solution)/shard_map/psum | solution.py:242
  534.0 11.6 all-to-all-done.1
  549.3 33.7 %gather_fusion.1 = bf16[8192,256]{1,0:T(8,128)(2,1)} fusion(bf16[8193,256]{1,0:T(8,128)(2,1)} %concatenate.55, s32[8192]{0:T(1024)S(1)} %broadcast_clamp_fusion), kind=kCustom, calls=%fused_computation.1 | custom fusion | bytes 8421376 | tf_op jit(solution)/shard_map/gather | solution.py:277
  608.9 33.7 %gather_fusion.2 = bf16[8192,256]{1,0:T(8,128)(2,1)} fusion(bf16[8193,256]{1,0:T(8,128)(2,1)} %concatenate.56, s32[8192]{0:T(1024)S(1)} %get-tuple-element.96), kind=kCustom, calls=%fused_computation.2 | custom fusion | bytes 8421376 | tf_op jit(solution)/shard_map/gather | solution.py:286
  642.6 53.9 %all_to_all.21 = bf16[8,1024,256]{2,1,0:T(8,128)(2,1)S(1)} all-to-all(bf16[8,1024,256]{2,1,0:T(8,128)(2,1)} %bitcast.185), channel_id=1, replica_groups=mesh['dp'=2,'row'=4,'col'=4] {'dp','row'}, dimensions={0} | all-to-all | bytes 8388608 | tf_op jit(solution)/shard_map/all_to_all | solution.py:103
  709.4 11.5 multiply_convert_fusion
  751.3 47.4 %all-to-all-done.3 = bf16[8,1024,256]{2,1,0:T(8,128)(2,1)} async-done(((bf16[8,1024,256]{2,1,0:T(8,128)(2,1)}), bf16[8,1024,256]{2,1,0:T(8,128)(2,1)}, u32[]{:S(2)}, u32[]{:S(2)}) %all-to-all-start.3) | async-done | bytes 4194336 | tf_op jit(solution)/shard_map/all_to_all | solution.py:108
  802.5 33.9 %gather_fusion.3 = bf16[8192,256]{1,0:T(8,128)(2,1)} fusion(bf16[8193,256]{1,0:T(8,128)(2,1)} %concatenate.57, s32[8192]{0:T(1024)S(1)} %broadcast_clamp_fusion), kind=kCustom, calls=%fused_computation.3 | custom fusion | bytes 8421376 | tf_op jit(solution)/shard_map/gather | solution.py:319
  849.3 46.3 %all-gather.9.cloned.1.call-done = bf16[4096,256]{1,0:T(8,128)(2,1)} async-done(((bf16[1024,256]{1,0:T(8,128)(2,1)}), bf16[4096,256]{1,0:T(8,128)(2,1)}) %all-gather.9.cloned.1.call-update) | async-done | bytes 2097168 | tf_op jit(solution)/shard_map/all_gather | solution.py:86
  899.4 29.1 %reduce-scatter.9.cloned.1.call-done = bf16[1024,256]{1,0:T(8,128)(2,1)} async-done(((bf16[4096,256]{1,0:T(8,128)(2,1)}), bf16[1024,256]{1,0:T(8,128)(2,1)}) %reduce-scatter.9.cloned.1.call-update) | async-done | bytes 524304 | tf_op jit(solution)/shard_map/reduce_scatter | solution.py:336
  938.4 13.0 fusion
  992.0 14.4 all-gather.11.cloned.1.call-done
  1025.5 413.5 %all-reduce.14.cloned.1.call-done = (bf16[4,1024,512]{2,1,0:T(8,128)(2,1)}, bf16[4,1024,512]{2,1,0:T(8,128)(2,1)}, bf16[4,512,1024]{2,1,0:T(8,128)(2,1)}) async-done(((bf16[4,1024,512]{2,1,0:T(8,128)(2,1)}, bf16[4,1024,512]{2,1,0:T(8,128)(2,1)}, bf16[4,512,1024]{2,1,0:T(8,128)(2,1)}), (bf16[4,1024,512]{2,1,0:T(8,128)(2,1)}, bf16[4,1024,512]{2,1,0:T(8,128)(2,1)}, ...) | async-done | bytes 12582928 | tf_op jit(solution)/shard_map/psum | solution.py:377
  1455.0 11.7 all-reduce.16.cloned.1.call-done
  1470.2 75.6 %reduce-scatter.11.cloned.1.call-done = f32[1024,256]{1,0:T(8,128)} async-done(((f32[4096,256]{1,0:T(8,128)}), f32[1024,256]{1,0:T(8,128)}) %reduce-scatter.11.cloned.1.call-update) | async-done | bytes 1048592 | tf_op jit(solution)/shard_map/reduce_scatter | solution.py:94
  1553.6 18.3 %all-reduce.4 = (bf16[256]{0:T(256)(128)(2,1)S(1)}, bf16[256]{0:T(256)(128)(2,1)S(1)}, bf16[256,32]{0,1:T(8,128)(2,1)S(1)}) all-reduce(bf16[256]{0:T(256)(128)(2,1)S(1)} %get-tuple-element.53, bf16[256]{0:T(256)(128)(2,1)S(1)} %get-tuple-element.51, ...), channel_id=1, replica_groups=mesh['dp'=2,'row'=4,'col'=4] {'col'}, use_global_device_ids=true, to_apply=%region_28.29 | all-reduce | flops 8704 | bytes 34816 | tf_op jit(solution)/shard_map/psum | solution.py:381
  (274 shorter events, 340.6 us)
Async XLA Ops:
  7.2 202.4 %copy-start = (bf16[2,128,256]{2,1,0:T(8,128)(2,1)S(1)}, bf16[2,128,256]{2,1,0:T(8,128)(2,1)}, u32[]{:S(2)}) copy-start(bf16[2,128,256]{2,1,0:T(8,128)(2,1)} %param.16) | copy-start | bytes 393220
  7.2 58.0 %all-gather.5.cloned.1.call-start = ((), (), s32[]{:S(2)}) async-start(), calls=%async_computation.8 | async-start | bytes 2621440 | tf_op jit(solution)/shard_map/all_gather | solution.py:86
  17.6 123.2 %reduce-scatter.5.cloned.1.call-start = ((), (), s32[]{:S(2)}) async-start(), calls=%async_computation.9 | async-start | bytes 10485760 | tf_op jit(solution)/shard_map/reduce_scatter | solution.py:210
  18.7 52.7 %copy-start.16 = (bf16[32,8,2,256]{3,1,2,0:T(8,128)(2,1)}, bf16[32,8,2,256]{3,1,2,0:T(8,128)(2,1)S(1)}, u32[]{:S(2)}) copy-start(bf16[32,8,2,256]{3,1,2,0:T(8,128)(2,1)S(1)} %copy.106) | copy-start | bytes 786436
  71.4 138.2 %all-gather.7.cloned.1.call-start = ((), (), s32[]{:S(2)}) async-start(), calls=%async_computation.10 | async-start | bytes 2621440 | tf_op jit(solution)/shard_map/all_gather | solution.py:90
  72.0 80.5 %copy-start.12 = (f32[1024,32]{0,1:T(8,128)}, f32[1024,32]{0,1:T(8,128)S(1)}, u32[]{:S(2)}) copy-start(f32[1024,32]{0,1:T(8,128)S(1)} %get-tuple-element.100) | copy-start | bytes 393220
  72.0 80.5 %copy-start.14 = (f32[1024,32]{0,1:T(8,128)}, f32[1024,32]{0,1:T(8,128)S(1)}, u32[]{:S(2)}) copy-start(f32[1024,32]{0,1:T(8,128)S(1)} %get-tuple-element.101) | copy-start | bytes 393220
  177.6 178.2 %reduce-scatter.7.cloned.1.call-start = ((), (), s32[]{:S(2)}) async-start(), calls=%async_computation.11 | async-start | bytes 5242880 | tf_op jit(solution)/shard_map/reduce_scatter | solution.py:94
  276.5 79.3 %copy-start.2 = (bf16[1024,256]{1,0:T(8,128)(2,1)S(1)}, bf16[1024,256]{1,0:T(8,128)(2,1)}, u32[]{:S(2)}) copy-start(bf16[1024,256]{1,0:T(8,128)(2,1)} %param.13) | copy-start | bytes 1572868
  491.8 53.8 %all-to-all-start.1 = ((bf16[8,1024,256]{2,1,0:T(8,128)(2,1)}), bf16[8,1024,256]{2,1,0:T(8,128)(2,1)}, u32[]{:S(2)}, u32[]{:S(2)}) async-start(bf16[8,1024,256]{2,1,0:T(8,128)(2,1)} %bitcast.180), calls=%async_computation.3 | async-start | bytes 8388608 | tf_op jit(solution)/shard_map/all_to_all | solution.py:108
  497.8 35.1 %all-reduce.12.cloned.1.call-start = ((), (), s32[]{:S(2)}) async-start(), calls=%async_computation.12 | async-start | bytes 131072 | tf_op jit(solution)/shard_map/psum | solution.py:242
  745.1 53.6 %all-to-all-start.3 = ((bf16[8,1024,256]{2,1,0:T(8,128)(2,1)}), bf16[8,1024,256]{2,1,0:T(8,128)(2,1)}, u32[]{:S(2)}, u32[]{:S(2)}) async-start(bf16[8,1024,256]{2,1,0:T(8,128)(2,1)} %bitcast.181), calls=%async_computation.5 | async-start | bytes 8388608 | tf_op jit(solution)/shard_map/all_to_all | solution.py:108
  751.0 144.7 %all-gather.9.cloned.1.call-start = ((), (), s32[]{:S(2)}) async-start(), calls=%async_computation.13 | async-start | bytes 2621440 | tf_op jit(solution)/shard_map/all_gather | solution.py:86
  849.3 50.1 %copy-start.37 = (f32[2,2,1024]{2,1,0:T(2,128)S(1)}, f32[2,2,1024]{2,1,0:T(2,128)}, u32[]{:S(2)}) copy-start(f32[2,2,1024]{2,1,0:T(2,128)} %copy-done.36) | copy-start | bytes 49156
  849.3 50.1 %copy-start.39 = (f32[2,2,1024]{2,1,0:T(2,128)S(1)}, f32[2,2,1024]{2,1,0:T(2,128)}, u32[]{:S(2)}) copy-start(f32[2,2,1024]{2,1,0:T(2,128)} %copy-done.38) | copy-start | bytes 49156
  849.3 79.2 %reduce-scatter.9.cloned.1.call-start = ((), (), s32[]{:S(2)}) async-start(), calls=%async_computation.14 | async-start | bytes 2621440 | tf_op jit(solution)/shard_map/reduce_scatter | solution.py:336
  899.3 107.1 %all-gather.11.cloned.1.call-start = ((), (), s32[]{:S(2)}) async-start(), calls=%async_computation.15 | async-start | bytes 5242880 | tf_op jit(solution)/shard_map/all_gather | solution.py:90
  971.8 467.3 %all-reduce.14.cloned.1.call-start = ((), (), s32[]{:S(2)}) async-start(), calls=%async_computation.17 | async-start | bytes 25165824 | tf_op jit(solution)/shard_map/psum | solution.py:377
  988.3 478.4 %all-reduce.16.cloned.1.call-start = ((), (), s32[]{:S(2)}) async-start(), calls=%async_computation.18 | async-start | bytes 786432 | tf_op jit(solution)/shard_map/psum | solution.py:385
  1011.3 534.6 %reduce-scatter.11.cloned.1.call-start = ((), (), s32[]{:S(2)}) async-start(), calls=%async_computation.16 | async-start | bytes 5242880 | tf_op jit(solution)/shard_map/reduce_scatter | solution.py:94
  1450.5 95.3 %copy-start.3 = (bf16[1024,256]{1,0:T(8,128)(2,1)S(1)}, bf16[1024,256]{1,0:T(8,128)(2,1)}, u32[]{:S(2)}) copy-start(bf16[1024,256]{1,0:T(8,128)(2,1)} %param.13) | copy-start | bytes 1572868
  1450.5 95.3 %copy-start.35 = (f32[1024]{0:T(1024)S(1)}, f32[1024]{0:T(1024)}, u32[]{:S(2)}) copy-start(f32[1024]{0:T(1024)} %copy-done.34) | copy-start | bytes 12292
  1450.5 95.3 %copy-start.45 = (f32[256]{0:T(256)S(1)}, f32[256]{0:T(256)}, u32[]{:S(2)}) copy-start(f32[256]{0:T(256)} %copy-done.44) | copy-start | bytes 3076
  1450.5 103.1 %copy-start.41 = (f32[1024]{0:T(1024)S(1)}, f32[1024]{0:T(1024)}, u32[]{:S(2)}) copy-start(f32[1024]{0:T(1024)} %copy-done.40) | copy-start | bytes 12292
  (46 other events, 392.1 us)
Sparse Core Ops, SparseCore 0:
  17.8 47.3 all-gather.4
  71.5 69.2 reduce-scatter.4
  177.7 22.5 all-gather.6
  214.1 77.9 reduce-scatter.6
  501.2 31.6 all-reduce.11
  849.4 46.2 all-gather.8
  899.4 28.9 reduce-scatter.8
  971.9 34.4 all-gather.10
  1010.4 428.6 all-reduce.13
  1441.8 24.8 all-reduce.15
  1469.1 76.7 reduce-scatter.10
where the time goes:
time: 1610 us; the launch traced here: 1590 us
  waiting for transfers between devices  797 us (50%)
  local copies, waits for them, and re-layouts  379 us (24%)
  blocking collectives  168 us (10%)
  matrix products  141 us (9%)
  other arithmetic  79.4 us (5%)
    psum x1, waiting for transfers between devices, on_device(): lax.psum(grad_gate_local.astype(jnp.bfloat16), 'col').astype(jnp.float32)  413 us
    all_to_all x2, blocking collectives, to_experts(): lax.all_to_all(outgoing, ('dp', 'row'), split_axis=0, concat_axis=0, tile...  106 us
    all_gather x2, waiting for transfers between devices, tokens_by_col(): return lax.all_gather(values, 'col', axis=0, tiled=True)  92.8 us
    reduce_scatter x2, waiting for transfers between devices, col_scatter(): lax.psum_scatter(term_fn(jnp.int32(0), keep_rows * lax.axis_size('col')),...  75.7 us
    reduce_scatter x1, waiting for transfers between devices, on_device(): lax.psum_scatter(jnp.dot(picked, qkv_flat, preferred_element_type=jnp.flo...  67.2 us
    all_to_all x2, waiting for transfers between devices, from_experts(): lax.all_to_all(outgoing, ('dp', 'row'), split_axis=0, concat_axis=0, tile...  59 us
    gather x2, local copies, waits for them, and re-layouts, one_block(): sorted_experts = experts_row[by_order]  48 us
    gather x1, local copies, waits for them, and re-layouts, one_block(): return sorted_rank[order_row]  48 us
  transfers between devices with their start and end apart: 13, of which 11 were waited for; matrix products, arithmetic and copies ran while one was open for 15% of the time, Pallas kernels for 0%

commit v1 on v0

--- a/solution.py
+++ b/solution.py
@@ -1,6 +1,11 @@
+import functools
+
 import jax
 import jax.numpy as jnp
+import numpy as np
 from jax import lax
+from jax.experimental import pallas as pl
+from jax.experimental.pallas import tpu as pltpu
 from jax.sharding import PartitionSpec as P
 
 D = 1024
@@ -401,38 +406,514 @@
         col_sums[2],
     )
 
+WINDOW = 512
+BLOCK_Q = 256
+LANES = 128
+F32 = jnp.float32
+LOW = jnp.bfloat16
+VMEM_BYTES = 67_000_000
+
+
+def dot_nn(a, b):
+    return jnp.dot(a, b, preferred_element_type=F32)
+
+
+def dot_nt(a, b):
+    return lax.dot_general(a, b, (((1,), (1,)), ((), ())), preferred_element_type=F32)
+
+
+def dot_tn(a, b):
+    return lax.dot_general(a, b, (((0,), (0,)), ((), ())), preferred_element_type=F32)
+
+
+def rope_lanes(length):
+    positions = np.arange(length, dtype=np.float32)
+    frequency = (ROPE_BASE ** (-2.0 * np.arange(HD // 2, dtype=np.float32) / HD)).astype(np.float32)
+    angles = (positions[:, None] * frequency[None, :]).astype(np.float32)
+    cosine, sine = np.cos(angles), np.sin(angles)
+    signed = np.concatenate([-sine, sine], axis=1)
+    double = np.concatenate([cosine, cosine], axis=1)
+    ones, zeros = np.ones_like(double), np.zeros_like(double)
+    return np.stack(
+        [
+            np.concatenate([double, double], axis=1),
+            np.concatenate([signed, signed], axis=1),
+            np.concatenate([double, ones], axis=1),
+            np.concatenate([signed, zeros], axis=1),
+        ]
+    ).astype(np.float32)
+
+
+def swap_halves(values):
+    half = HD // 2
+    lane = lax.broadcasted_iota(jnp.int32, values.shape, 1)
+    ahead = pltpu.roll(values, LANES - half, 1)
+    behind = pltpu.roll(values, half, 1)
+    return jnp.where(lane % HD < half, ahead, behind)
+
+
+def window_mask(seg_col, seg_row, q_start, k_start):
+    shape = (seg_col.shape[0], seg_row.shape[1])
+    q_at = lax.broadcasted_iota(jnp.int32, shape, 0) + q_start
+    k_at = lax.broadcasted_iota(jnp.int32, shape, 1) + k_start
+    return (q_at >= k_at) & (seg_col == seg_row)
+
+
+def attend_forward_kernel(
+    h_ref, gain_ref, w_ref, seg_col_ref, seg_row_ref, tab_ref,
+    mixed_ref, normed_ref, q_ref, k_ref, v_ref, lse_ref,
+):
+    parts, length, width = h_ref.shape
+    kv_heads = k_ref.shape[0]
+    features = parts * width
+
+    @pl.loop(0, length // BLOCK_Q)
+    def _(chunk):
+        rows = pl.ds(pl.multiple_of(chunk * BLOCK_Q, BLOCK_Q), BLOCK_Q)
+        total = jnp.zeros((BLOCK_Q, 1), F32)
+        for part in range(parts):
+            piece = h_ref[part, rows, :].astype(F32)
+            total = total + jnp.sum(piece * piece, axis=1, keepdims=True)
+        rstd = lax.rsqrt(total / features + EPSILON)
+        for part in range(parts):
+            piece = h_ref[part, rows, :].astype(F32)
+            normed_ref[rows, part * width : (part + 1) * width] = (
+                piece * rstd * gain_ref[part]
+            ).astype(LOW)
+        qkv = dot_nn(normed_ref[rows, :], w_ref[...])
+        for head in range(kv_heads):
+            base = head * 4 * HD
+            queries = qkv[:, base : base + LANES]
+            queries = queries * tab_ref[0, rows, :] + swap_halves(queries) * tab_ref[1, rows, :]
+            others = qkv[:, base + LANES : base + 2 * LANES]
+            others = others * tab_ref[2, rows, :] + swap_halves(others) * tab_ref[3, rows, :]
+            q_ref[2 * head, rows, :] = queries[:, :HD].astype(LOW)
+            q_ref[2 * head + 1, rows, :] = queries[:, HD:].astype(LOW)
+            k_ref[head, rows, :] = others[:, :HD].astype(LOW)
+            v_ref[head, rows, :] = others[:, HD:].astype(LOW)
+
+    scale = HD**-0.5
+    lane = lax.broadcasted_iota(jnp.int32, (BLOCK_Q, LANES), 1)
+    for block in range(length // BLOCK_Q):
+        q_start = block * BLOCK_Q
+        k_start = max(0, q_start - WINDOW)
+        q_rows, k_rows = slice(q_start, q_start + BLOCK_Q), slice(k_start, q_start + BLOCK_Q)
+        mask = window_mask(seg_col_ref[q_rows, :], seg_row_ref[:, k_rows], q_start, k_start)
+        logs = jnp.zeros((BLOCK_Q, LANES), F32)
+        for head in range(2 * kv_heads):
+            scores = dot_nt(q_ref[head, q_rows, :], k_ref[head // 2, k_rows, :]) * scale
+            scores = jnp.where(mask, scores, NEG_LARGE)
+            top = jnp.max(scores, axis=1, keepdims=True)
+            weights = jnp.exp(scores - top)
+            total = jnp.sum(weights, axis=1, keepdims=True)
+            out = dot_nn(weights.astype(LOW), v_ref[head // 2, k_rows, :]) / total
+            mixed_ref[q_rows, head * HD : (head + 1) * HD] = out.astype(LOW)
+            logs = jnp.where(lane == head, top + jnp.log(total), logs)
+        lse_ref[q_rows, :] = logs
+
+
+def attend_backward_kernel(
+    gb_ref, wo_ref, wq_ref, normed_ref, mixed_ref, q_ref, k_ref, v_ref, lse_ref, seg_col_ref, seg_row_ref, tab_ref,
+    back_ref, grads_ref,
+    gm_ref, dqkv_ref, dk_ref, dv_ref, low_ref,
+):
+    parts, length, width = gb_ref.shape
+    kv_heads = k_ref.shape[0]
+    scale = HD**-0.5
+    dk_ref[...] = jnp.zeros_like(dk_ref)
+    dv_ref[...] = jnp.zeros_like(dv_ref)
+
+    @pl.loop(0, length // BLOCK_Q)
+    def _(chunk):
+        rows = pl.ds(pl.multiple_of(chunk * BLOCK_Q, BLOCK_Q), BLOCK_Q)
+        total = dot_nt(gb_ref[0, rows, :], wo_ref[0])
+        for part in range(1, parts):
+            total = total + dot_nt(gb_ref[part, rows, :], wo_ref[part])
+        for head in range(2 * kv_heads):
+            gm_ref[head, rows, :] = total[:, head * HD : (head + 1) * HD].astype(LOW)
+
+    for block in range(length // BLOCK_Q):
+        q_start = block * BLOCK_Q
+        k_start = max(0, q_start - WINDOW)
+        q_rows, k_rows = slice(q_start, q_start + BLOCK_Q), slice(k_start, q_start + BLOCK_Q)
+        mask = window_mask(seg_col_ref[q_rows, :], seg_row_ref[:, k_rows], q_start, k_start)
+        logs = lse_ref[q_rows, :]
+        for kv in range(kv_heads):
+            keys, vals = k_ref[kv, k_rows, :], v_ref[kv, k_rows, :]
+            for head in (2 * kv, 2 * kv + 1):
+                queries, grad = q_ref[head, q_rows, :], gm_ref[head, q_rows, :]
+                scores = dot_nt(queries, keys) * scale
+                weights = jnp.where(mask, jnp.exp(scores - logs[:, head : head + 1]), 0.0)
+                grad_weights = dot_nt(grad, vals)
+                inner = jnp.sum(weights * grad_weights, axis=1, keepdims=True)
+                grad_scores = (weights * (grad_weights - inner)).astype(LOW)
+                dv_ref[kv, k_rows, :] += dot_tn(weights.astype(LOW), grad)
+                dk_ref[kv, k_rows, :] += dot_tn(grad_scores, queries)
+                lanes = kv * 4 * HD + (head % 2) * HD
+                dqkv_ref[q_rows, lanes : lanes + HD] = dot_nn(grad_scores, keys) * scale
+
+    @pl.loop(0, length // BLOCK_Q)
+    def _(chunk):
+        rows = pl.ds(pl.multiple_of(chunk * BLOCK_Q, BLOCK_Q), BLOCK_Q)
+        for kv in range(kv_heads):
+            base = kv * 4 * HD
+            queries = dqkv_ref[rows, base : base + LANES]
+            queries = queries * tab_ref[0, rows, :] - swap_halves(queries) * tab_ref[1, rows, :]
+            others = jnp.concatenate([dk_ref[kv, rows, :] * scale, dv_ref[kv, rows, :]], axis=1)
+            others = others * tab_ref[2, rows, :] - swap_halves(others) * tab_ref[3, rows, :]
+            low_ref[rows, base : base + LANES] = queries.astype(LOW)
+            low_ref[rows, base + LANES : base + 2 * LANES] = others.astype(LOW)
+        for part in range(parts):
+            back_ref[part, rows, :] = dot_nt(low_ref[rows, :], wq_ref[part]).astype(LOW)
+
+    columns = low_ref.shape[1]
+    for part in range(parts):
+        grads_ref[part, :, :columns] = dot_tn(
+            normed_ref[:, part * width : (part + 1) * width], low_ref[...]
+        ).astype(LOW)
+        grads_ref[part, :, columns:] = dot_tn(mixed_ref[...], gb_ref[part]).astype(LOW)
+
+
+def moe_kernel(
+    counts, res_hbm, cot_hbm, rk_ref, gain_ref, router_ref, wg_ref, wu_ref, wd_ref,
+    y_hbm, pb_hbm, gg_ref, gates_out_ref, logits_out_ref, dg_ref, du_ref, dd_ref,
+    res_ref, cot_ref, x_ref, gate_ref, pick_ref, eo_ref, back_ref, stage_ref, sems, out_sem,
+):
+    dp_count, row_count, col_count = counts
+    blocks = dp_count * col_count
+    my_dp, my_row, my_col = lax.axis_index("dp"), lax.axis_index("row"), lax.axis_index("col")
+    experts, features, hidden_width = wg_ref.shape
+    _, parts, length, width = res_hbm.shape
+    capacity = pick_ref.shape[0] // experts
+    first_expert = (my_dp * row_count + my_row) * experts
+
+    def block_of(step):
+        other = step - dp_count
+        far = dp_count <= step
+        dp_at = jnp.where(far, other // (col_count - 1), step)
+        col_at = jnp.where(far, lax.rem(my_col + 1 + lax.rem(other, col_count - 1), col_count), my_col)
+        return dp_at * col_count + col_at
+
+    def fetch(step):
+        b = block_of(step)
+        slot = lax.rem(step, 2)
+        return (
+            pltpu.make_async_copy(res_hbm.at[b], res_ref, sems.at[0]),
+            pltpu.make_async_copy(cot_hbm.at[b], cot_ref.at[slot], sems.at[1 + slot]),
+        )
+
+    for copy in fetch(0):
+        copy.start()
+    dg_ref[...] = jnp.zeros_like(dg_ref)
+    du_ref[...] = jnp.zeros_like(du_ref)
+    dd_ref[...] = jnp.zeros_like(dd_ref)
+
+    @pl.loop(0, blocks)
+    def _(step):
+        b = block_of(step)
+        slot = lax.rem(step, 2)
+        for copy in fetch(step):
+            copy.wait()
+
+        @pl.loop(0, length // BLOCK_Q)
+        def _(chunk):
+            rows = pl.ds(pl.multiple_of(chunk * BLOCK_Q, BLOCK_Q), BLOCK_Q)
+            total = jnp.zeros((BLOCK_Q, 1), F32)
+            for part in range(parts):
+                piece = res_ref[part, rows, :].astype(F32)
+                total = total + jnp.sum(piece * piece, axis=1, keepdims=True)
+            rstd = lax.rsqrt(total / features + EPSILON)
+            for part in range(parts):
+                piece = res_ref[part, rows, :].astype(F32)
+                x_ref[rows, part * width : (part + 1) * width] = (
+                    piece * rstd * gain_ref[part]
+                ).astype(LOW)
+
+        @pl.when(step + 1 < blocks)
+        def _():
+            for copy in fetch(step + 1):
+                copy.start()
+
+        logits = dot_nt(router_ref[...], x_ref[...])
+        chosen = rk_ref[b] >= 0.0
+        shown = jnp.where(chosen, logits, NEG_LARGE)
+        weights = jnp.where(chosen, jnp.exp(shown - jnp.max(shown, axis=0, keepdims=True)), 0.0)
+        gates = weights / jnp.sum(weights, axis=0, keepdims=True)
+        gate_ref[...] = gates
+
+        @pl.when(step < dp_count)
+        def _():
+            gates_out_ref[step] = gates
+            logits_out_ref[step] = logits
+
+        @pl.loop(0, experts)
+        def _(e):
+            rank_row = rk_ref[b, pl.ds(first_expert + e, 1), :]
+            gate_row = gate_ref[pl.ds(first_expert + e, 1), :]
+            at = lax.broadcasted_iota(jnp.int32, (capacity, length), 0).astype(F32)
+            here = at == rank_row
+            pick = here.astype(F32).astype(LOW)
+            gate_slot = jnp.sum(jnp.where(here, gate_row, 0.0), axis=1, keepdims=True)
+            x = dot_nn(pick, x_ref[...]).astype(LOW)
+            g = jnp.concatenate([dot_nn(pick, cot_ref[slot, part]) for part in range(parts)], axis=1)
+            pair_grad = (g * gate_slot).astype(LOW)
+            gate_pre = dot_nn(x, wg_ref[e])
+            up_pre = dot_nn(x, wu_ref[e])
+            sig = 1.0 / (1.0 + jnp.exp(-gate_pre))
+            silu = gate_pre * sig
+            hidden = (silu * up_pre).astype(LOW)
+            grad_hidden = dot_nt(pair_grad, wd_ref[e])
+            grad_gate = (grad_hidden * up_pre * (sig * (1.0 + gate_pre * (1.0 - sig)))).astype(LOW)
+            grad_up = (grad_hidden * silu).astype(LOW)
+
+            @pl.when(step < dp_count)
+            def _():
+                slots = pl.ds(pl.multiple_of(e * capacity, capacity), capacity)
+                out = dot_nn(hidden, wd_ref[e]).astype(LOW).astype(F32)
+                along = jnp.sum(g * out, axis=1, keepdims=True)
+                gg_ref[step, pl.ds(e, 1), :] = jnp.sum(
+                    jnp.where(here, along, 0.0), axis=0, keepdims=True
+                )
+                pick_ref[slots, :] = pick
+                eo_ref[slots, :] = (out * gate_slot).astype(LOW)
+                back_ref[slots, :] = (
+                    dot_nt(grad_gate, wg_ref[e]) + dot_nt(grad_up, wu_ref[e])
+                ).astype(LOW)
+
+            dd_ref[e] += dot_tn(hidden, pair_grad)
+            dg_ref[e] += dot_tn(x, grad_gate)
+            du_ref[e] += dot_tn(x, grad_up)
+
+        @pl.when(step < dp_count)
+        def _():
+            for source, target in ((back_ref, pb_hbm), (eo_ref, y_hbm)):
+                for part in range(parts):
+                    cols = slice(part * width, (part + 1) * width)
+                    stage_ref[part] = dot_tn(pick_ref[...], source[:, cols]).astype(LOW)
+                copy = pltpu.make_async_copy(stage_ref, target.at[step], out_sem)
+                copy.start()
+                copy.wait()
+
+
+def fast_device(
+    hidden_in, norm_gain, w_qkv, w_out, ffn_gain, router, w_gate, w_up, w_down, cotangent,
+    segment_ids, expert_ids, pair_order,
+):
+    dp_count, row_count, col_count = (lax.axis_size(name) for name in ("dp", "row", "col"))
+    my_dp, my_row, my_col = (lax.axis_index(name) for name in ("dp", "row", "col"))
+    length, width = hidden_in.shape
+    kv_local = w_qkv.shape[1]
+    head_width = kv_local * (HQ // HK) * HD
+    qkv_width = kv_local * (HQ // HK + 2) * HD
+    exp_local, _, hidden_width = w_gate.shape
+    capacity = length * TOP // EXPERTS
+    blocks = dp_count * col_count
+    vmem = pl.BlockSpec(memory_space=pltpu.VMEM)
+    hbm = pl.BlockSpec(memory_space=pl.ANY)
+    params = pltpu.CompilerParams(vmem_limit_bytes=VMEM_BYTES)
+
+    ids_t, order_t = expert_ids.T, pair_order.T
+    experts_here = EXPERTS // row_count
+    mine = my_row * experts_here + jnp.arange(experts_here, dtype=jnp.int32)
+    match = ids_t[None, :, :] == mine[:, None, None]
+    chosen = jnp.any(match, axis=1)
+    orders = jnp.sum(jnp.where(match, order_t[None], 0), axis=1)
+    orders = jnp.where(chosen, orders, length * TOP)
+    ranks = jnp.sum((orders[:, :, None] < orders[:, None, :]).astype(jnp.int32), axis=1)
+    ranks = jnp.where(chosen, jnp.minimum(ranks, capacity), -1).astype(F32)
+    rank_all = lax.all_gather(ranks, ("dp", "row", "col"), axis=0)
+    rank_all = (
+        rank_all.reshape(dp_count, row_count, col_count, experts_here, length)
+        .transpose(0, 2, 1, 3, 4)
+        .reshape(blocks, EXPERTS, length)
+    )
+    cot_all = lax.all_gather(cotangent, ("dp", "col", "row"), axis=0).reshape(
+        blocks, row_count, length, width
+    )
+
+    own = jnp.concatenate([w_qkv.reshape(width, qkv_width), w_out.reshape(head_width, width)], axis=1)
+    own_cols = lax.all_gather(own, "col", axis=0)
+    own_rows = lax.all_to_all(own_cols, "row", split_axis=0, concat_axis=0, tiled=True)
+    wq_rows = own_rows[:, :, :qkv_width]
+    wo_rows = own_rows[:, :, qkv_width:]
+    wo_cols = own_cols[:, :, qkv_width:]
+    gains = lax.all_gather(
+        jnp.concatenate([norm_gain[None], ffn_gain[None], router.T], axis=0), "row", axis=0
+    ).astype(F32)
+    gain_one, gain_two = gains[:, 0:1], gains[:, 1:2]
+    router_t = gains[:, 2:].transpose(1, 0, 2).reshape(EXPERTS, -1).astype(LOW)
+    segments = lax.dynamic_index_in_dim(
+        lax.all_gather(segment_ids, "row", axis=0), my_col, axis=0, keepdims=False
+    )
+    seg_row, seg_col = segments.reshape(1, length), segments.reshape(length, 1)
+    tables = jnp.asarray(rope_lanes(length))
+
+    hidden_all = lax.all_gather(hidden_in, "row", axis=0)
+    mixed, normed_one, query_rot, key_rot, value_low, logs = pl.pallas_call(
+        attend_forward_kernel,
+        out_shape=(
+            jax.ShapeDtypeStruct((length, head_width), LOW),
+            jax.ShapeDtypeStruct((length, D), LOW),
+            jax.ShapeDtypeStruct((2 * kv_local, length, HD), LOW),
+            jax.ShapeDtypeStruct((kv_local, length, HD), LOW),
+            jax.ShapeDtypeStruct((kv_local, length, HD), LOW),
+            jax.ShapeDtypeStruct((length, LANES), F32),
+        ),
+        in_specs=[vmem] * 6,
+        out_specs=[vmem] * 6,
+        compiler_params=params,
+        name="attend_forward",
+    )(hidden_all, gain_one, wq_rows.reshape(D, qkv_width), seg_col, seg_row, tables)
+
+    mixed_all = lax.all_gather(mixed, "row", axis=0)
+    resid_in = hidden_in.astype(F32)
+    branch = jnp.einsum("rtc,rcd->td", mixed_all, wo_cols, preferred_element_type=F32)
+    resid_mid = resid_in + branch
+    resid_low = resid_mid.astype(LOW)
+    resid_all = lax.all_gather(resid_low, ("dp", "col", "row"), axis=0).reshape(
+        blocks, row_count, length, width
+    )
+
+    y_part, pb_part, gg_part, gates_plane, logits_plane, grad_gate, grad_up, grad_down = pl.pallas_call(
+        functools.partial(moe_kernel, (dp_count, row_count, col_count)),
+        out_shape=(
+            jax.ShapeDtypeStruct((dp_count, row_count, length, width), LOW),
+            jax.ShapeDtypeStruct((dp_count, row_count, length, width), LOW),
+            jax.ShapeDtypeStruct((dp_count, exp_local, length), F32),
+            jax.ShapeDtypeStruct((dp_count, EXPERTS, length), F32),
+            jax.ShapeDtypeStruct((dp_count, EXPERTS, length), F32),
+            jax.ShapeDtypeStruct(w_gate.shape, F32),
+            jax.ShapeDtypeStruct(w_up.shape, F32),
+            jax.ShapeDtypeStruct(w_down.shape, F32),
+        ),
+        in_specs=[hbm, hbm] + [vmem] * 6,
+        out_specs=[hbm, hbm] + [vmem] * 6,
+        scratch_shapes=[
+            pltpu.VMEM((row_count, length, width), LOW),
+            pltpu.VMEM((2, row_count, length, width), LOW),
+            pltpu.VMEM((length, D), LOW),
+            pltpu.VMEM((EXPERTS, length), F32),
+            pltpu.VMEM((exp_local * capacity, length), LOW),
+            pltpu.VMEM((exp_local * capacity, D), LOW),
+            pltpu.VMEM((exp_local * capacity, D), LOW),
+            pltpu.VMEM((row_count, length, width), LOW),
+            pltpu.SemaphoreType.DMA((3,)),
+            pltpu.SemaphoreType.DMA,
+        ],
+        compiler_params=params,
+        name="experts",
+    )(resid_all, cot_all, rank_all, gain_two, router_t, w_gate, w_up, w_down)
+
+    grad_expert = lax.psum_scatter(
+        pb_part.reshape(-1, width), ("dp", "row"), scatter_dimension=0, tiled=True
+    ).astype(F32)
+    mixture = lax.psum_scatter(
+        y_part.reshape(-1, width), ("dp", "row"), scatter_dimension=0, tiled=True
+    ).astype(F32)
+    layer_out = (resid_mid + mixture).astype(LOW)
+
+    gg_all = lax.all_gather(gg_part, ("dp", "row"), axis=0)
+    gg = lax.dynamic_index_in_dim(gg_all, my_dp, axis=1, keepdims=False).reshape(EXPERTS, length)
+    gates = lax.dynamic_index_in_dim(gates_plane, my_dp, axis=0, keepdims=False)
+    inner_gate = jnp.sum(gates * gg, axis=0, keepdims=True)
+    grad_logits = gates * (gg - inner_gate)
+
+    gain_float = ffn_gain.astype(F32)
+    router_float = router.astype(F32)
+    block_all = lax.dynamic_index_in_dim(
+        resid_all, my_dp * col_count + my_col, axis=0, keepdims=False
+    ).astype(F32)
+    rstd_two = lax.rsqrt(jnp.sum(block_all * block_all, axis=(0, 2)) / D + EPSILON)[:, None]
+    grad_top = cotangent.astype(F32)
+    grad_normed = grad_expert + jnp.einsum("et,de->td", grad_logits, router_float)
+    normed_float = resid_mid * rstd_two * gain_float
+    grad_router = jnp.einsum("td,et->de", normed_float, grad_logits)
+    grad_gain_two = jnp.sum(grad_normed * resid_mid * rstd_two, axis=0)
+    scaled_two = grad_normed * gain_float
+    inner_two = lax.psum(jnp.sum(scaled_two * resid_mid, axis=1), "row")[:, None]
+    grad_resid = (
+        grad_top + rstd_two * scaled_two - resid_mid * (rstd_two * rstd_two * rstd_two * inner_two / D)
+    )
+    branch_all = lax.all_gather(grad_resid.astype(LOW), "row", axis=0)
+
+    back_part, grads_part = pl.pallas_call(
+        attend_backward_kernel,
+        out_shape=(
+            jax.ShapeDtypeStruct((row_count, length, width), LOW),
+            jax.ShapeDtypeStruct((row_count, width, qkv_width + width), LOW),
+        ),
+        in_specs=[vmem] * 12,
+        out_specs=[vmem] * 2,
+        scratch_shapes=[
+            pltpu.VMEM((2 * kv_local, length, HD), LOW),
+            pltpu.VMEM((length, qkv_width), F32),
+            pltpu.VMEM((kv_local, length, HD), F32),
+            pltpu.VMEM((kv_local, length, HD), F32),
+            pltpu.VMEM((length, qkv_width), LOW),
+        ],
+        compiler_params=params,
+        name="attend_backward",
+    )(
+        branch_all, wo_rows, wq_rows, normed_one, mixed, query_rot, key_rot, value_low, logs,
+        seg_col, seg_row, tables,
+    )
+    grad_normed_one = lax.psum_scatter(
+        back_part.reshape(-1, width), "row", scatter_dimension=0, tiled=True
+    ).astype(F32)
+    grads_own = lax.psum_scatter(
+        grads_part.reshape(row_count * width, -1), "col", scatter_dimension=0, tiled=True
+    )
+    swap = [(a * col_count + b, b * col_count + a) for a in range(row_count) for b in range(col_count)]
+    grads_own = lax.psum(lax.ppermute(grads_own, ("row", "col"), swap), "dp").astype(F32)
+    grad_qkv = grads_own[:, :qkv_width].reshape(w_qkv.shape)
+    grad_out = grads_own[:, qkv_width:].reshape(w_out.shape)
+
+    gain_first = norm_gain.astype(F32)
+    hid_float = hidden_all.astype(F32)
+    rstd_one = lax.rsqrt(jnp.sum(hid_float * hid_float, axis=(0, 2)) / D + EPSILON)[:, None]
+    grad_gain_one = jnp.sum(grad_normed_one * resid_in * rstd_one, axis=0)
+    scaled_one = grad_normed_one * gain_first
+    inner_one = lax.psum(jnp.sum(scaled_one * resid_in, axis=1), "row")[:, None]
+    grad_in = (
+        grad_resid + rstd_one * scaled_one - resid_in * (rstd_one * rstd_one * rstd_one * inner_one / D)
+    )
+    small = jnp.concatenate([grad_router.T, grad_gain_one[None], grad_gain_two[None]], axis=0)
+    small = lax.psum(small, ("dp", "col"))
+    return (
+        layer_out,
+        grad_in,
+        small[EXPERTS],
+        grad_qkv,
+        grad_out,
+        small[EXPERTS + 1],
+        small[:EXPERTS].T,
+        grad_gate,
+        grad_up,
+        grad_down,
+    )
+
 
 def solution(mesh):
-    placed = (
-        P(("dp", "col"), "row"),
-        P("row"),
-        P("row", "col", None),
-        P("col", None, "row"),
-        P("row"),
-        P("row", None),
-        P(("dp", "row"), None, None),
-        P(("dp", "row"), None, None),
-        P(("dp", "row"), None, None),
-        P(("dp", "col"), "row"),
-        P(("dp", "row"), None),
-        P(("dp", "col"), None),
-        P(("dp", "col"), None),
-    )
-    return jax.shard_map(
-        on_device,
-        mesh=mesh,
-        in_specs=placed,
-        out_specs=(
-            P(("dp", "col"), "row"),
-            P(("dp", "col"), "row"),
-            P("row"),
-            P("row", "col", None),
-            P("col", None, "row"),
-            P("row"),
-            P("row", None),
-            P(("dp", "row"), None, None),
-            P(("dp", "row"), None, None),
-            P(("dp", "row"), None, None),
-        ),
-        check_vma=False,
-    )
+    token = P(("dp", "col"), "row")
+    routed = P(("dp", "col"), None)
+    expert = P(("dp", "row"), None, None)
+    wide, tall = P("row", "col", None), P("col", None, "row")
+    row = P("row")
+    square = P("row", None)
+
+    def step(*arrays):
+        length = arrays[10].shape[1]
+        tokens_here = arrays[0].shape[0] // (mesh.shape["dp"] * mesh.shape["col"])
+        whole_sequence = tokens_here == length and mesh.shape["row"] == mesh.shape["col"]
+        return jax.shard_map(
+            fast_device if whole_sequence else on_device,
+            mesh=mesh,
+            in_specs=(
+                token, row, wide, tall, row, square, expert, expert, expert, token,
+                P(("dp", "row"), None), routed, routed,
+            ),
+            out_specs=(token, token, row, wide, tall, row, square, expert, expert, expert),
+            check_vma=False,
+        )(*arrays)
+
+    return step

time: 1610 us -> 876 us (0.54)
  local copies, waits for them, and re-layouts: 379 us -> 19.2 us
  waiting for transfers between devices: 797 us -> 505 us
  Pallas kernels: 0 us -> 197 us
  matrix products: 141 us -> 7.52 us
  blocking collectives: 168 us -> 95.7 us
  other arithmetic: 79.4 us -> 19.5 us
    psum x3 -> x1, waiting for transfers between devices: 458 us -> 17.8 us  [fast_device(): lax.psum(lax.ppermute(grads_own, ('row', 'col'), swap), 'dp').astype(F32)]
    all_gather x4 -> x7, waiting for transfers between devices: 107 us -> 357 us  [the longest x1 116 us: fast_device(): lax.all_gather(resid_low, ('dp', 'col', 'row'), axis=0)]
    gather x7 -> x0, local copies, waits for them, and re-layouts: 230 us -> none  [the longest x2 48 us: one_block(): sorted_experts = experts_row[by_order]]
    pallas_call x0 -> x3, Pallas kernels: none -> 197 us  [the longest x1 160 us: fast_device(): pl.pallas_call(functools.partial(moe_kernel, (dp_count, row_count, col_co...]
    dot_general x26 -> x3, matrix products: 141 us -> 7.52 us  [the longest x1 3.72 us: fast_device(): jnp.einsum('rtc,rcd->td', mixed_all, wo_cols, preferred_element_type=F32)]
    all_to_all x2 -> x0, blocking collectives: 106 us -> none  [to_experts(): lax.all_to_all(outgoing, ('dp', 'row'), split_axis=0, concat_axis=0, tile...]
    reduce_scatter x4, waiting for transfers between devices: 172 us -> 109 us  [the longest x1 38 us: fast_device(): lax.psum_scatter(pb_part.reshape(-1, width), ('dp', 'row'), scatter_dimen...]
    all_to_all x2 -> x1, waiting for transfers between devices: 59 us -> 0.01 us  [fast_device(): lax.all_to_all(own_cols, 'row', split_axis=0, concat_axis=0, tiled=True)]
  transfers between devices with their start and end apart: 13 -> 14, of which waited for: 11 -> 12; matrix products, arithmetic and copies ran while one was open for 15% -> 4% of each run, Pallas kernels for 0% -> 0%
where the time goes in v1:
time: 876 us; the launch traced here: 867 us
  waiting for transfers between devices  505 us (58%)
  Pallas kernels  197 us (22%)
  blocking collectives  95.7 us (11%)
  other arithmetic  19.5 us (2%)
  local copies, waits for them, and re-layouts  19.2 us (2%)
  between operations  15 us (2%)
    pallas_call x1, Pallas kernels, fast_device(): pl.pallas_call(functools.partial(moe_kernel, (dp_count, row_count, col_co...  160 us
    all_gather x1, waiting for transfers between devices, fast_device(): lax.all_gather(resid_low, ('dp', 'col', 'row'), axis=0)  116 us
    all_gather x1, waiting for transfers between devices, fast_device(): lax.all_gather(cotangent, ('dp', 'col', 'row'), axis=0)  114 us
    all_gather x1, waiting for transfers between devices, fast_device(): rank_all = lax.all_gather(ranks, ('dp', 'row', 'col'), axis=0)  53.5 us
    psum x1, blocking collectives, fast_device(): small = lax.psum(small, ('dp', 'col'))  38 us
    reduce_scatter x1, waiting for transfers between devices, fast_device(): lax.psum_scatter(pb_part.reshape(-1, width), ('dp', 'row'), scatter_dimen...  38 us
    all_gather x1, waiting for transfers between devices, fast_device(): own_cols = lax.all_gather(own, 'col', axis=0)  37.8 us
    reduce_scatter x1, waiting for transfers between devices, fast_device(): lax.psum_scatter(grads_part.reshape(row_count * width, -1), 'col', scatte...  36.6 us
  transfers between devices with their start and end apart: 14, of which 12 were waited for; matrix products, arithmetic and copies ran while one was open for 4% of the time, Pallas kernels for 0%

profile of v1, /device:TPU:2, one launch (start us, length us, event | category | flops | bytes accessed | tf_op | source)
XLA Modules:
  0.0 867.1 jit_solution(15346734654611563090)
XLA Ops:
  10.7 37.8 %all-gather.22.cloned.1.call-done = bf16[1024,768]{1,0:T(8,128)(2,1)} async-done(((bf16[256,768]{1,0:T(8,128)(2,1)}), bf16[1024,768]{1,0:T(8,128)(2,1)}) %all-gather.22.cloned.1.call-update) | async-done | bytes 1572880 | tf_op jit(solution)/shard_map/all_gather | solution.py:735
  48.6 4.1 all-to-all-start
  52.7 30.6 %all-gather.11 = s32[4,1,1024]{2,1,0:T(1,128)S(1)} all-gather(s32[1,1,1024]{2,1,0:T(1,128)S(1)} %bitcast.82), channel_id=5, replica_groups=mesh['dp'=2,'row'=4,'col'=4] {'row'}, dimensions={0}, use_global_device_ids=true | all-gather | bytes 20480 | tf_op jit(solution)/shard_map/all_gather | solution.py:746
  84.9 5.3 all-gather.10
  93.7 13.5 %attend_forward.1 = (bf16[1024,256]{1,0:T(8,128)(2,1)}, bf16[1024,1024]{1,0:T(8,128)(2,1)}, bf16[4,1024,64]{2,1,0:T(8,128)(2,1)}, bf16[2,1024,64]{2,1,0:T(8,128)...) custom-call(bf16[4,1024,256]{2,1,0:T(8,128)(2,1)} %bitcast.59, f32[4,1,256]{2,1,0:T(1,128)} %get-tuple-element.47.gain_ref, ...), custom_call_target="tpu_custom_call" | custom-call | tf_op jit(solution)/shard_map/attend_forward/pallas_call | solution.py:752
  108.4 3.9 convert_reduce_fusion
  113.6 14.3 %all-gather.24.cloned.1.call-done = bf16[4096,256]{1,0:T(8,128)(2,1)} async-done(((bf16[1024,256]{1,0:T(8,128)(2,1)}), bf16[4096,256]{1,0:T(8,128)(2,1)}) %all-gather.24.cloned.1.call-update) | async-done | bytes 2097168 | tf_op jit(solution)/shard_map/all_gather | solution.py:768
  127.9 3.7 fusion.23
  132.5 53.5 %all-gather.30.cloned.1.call-done = f32[256,1024]{1,0:T(8,128)} async-done(((f32[8,1024]{1,0:T(8,128)}), f32[256,1024]{1,0:T(8,128)}) %all-gather.30.cloned.1.call-update) | async-done | bytes 1048592 | tf_op jit(solution)/shard_map/all_gather | solution.py:724
  188.4 114.2 %all-gather.28.cloned.1.call-done = bf16[32768,256]{1,0:T(8,128)(2,1)} async-done(((bf16[1024,256]{1,0:T(8,128)(2,1)}), bf16[32768,256]{1,0:T(8,128)(2,1)}) %all-gather.28.cloned.1.call-update) | async-done | bytes 16777232 | tf_op jit(solution)/shard_map/all_gather | solution.py:730
  302.6 116.4 %all-gather.26.cloned.1.call-done = bf16[32768,256]{1,0:T(8,128)(2,1)} async-done(((bf16[1024,256]{1,0:T(8,128)(2,1)}), bf16[32768,256]{1,0:T(8,128)(2,1)}) %all-gather.26.cloned.1.call-update) | async-done | bytes 16777232 | tf_op jit(solution)/shard_map/all_gather | solution.py:773
  419.0 160.1 %experts.1 = (bf16[2,4,1024,256]{3,2,1,0:T(8,128)(2,1)}, bf16[2,4,1024,256]{3,2,1,0:T(8,128)(2,1)}, f32[2,4,1024]{2,1,0:T(4,128)}, f32[2,32,1024]{2,1,0:T(8,128)...) custom-call(bf16[8,4,1024,256]{3,2,1,0:T(8,128)(2,1)} %bitcast.55, ...), custom_call_target="tpu_custom_call" | custom-call | tf_op jit(solution)/shard_map/experts/pallas_call | solution.py:777
  579.8 8.7 %all-gather.8 = f32[16,4,1024]{2,1,0:T(4,128)S(1)} all-gather(f32[2,4,1024]{2,1,0:T(4,128)S(1)} %copy-done.18), channel_id=10, replica_groups=mesh['dp'=2,'row'=4,'col'=4] {'dp','row'}, dimensions={0}, use_global_device_ids=true | all-gather | bytes 294912 | tf_op jit(solution)/shard_map/all_gather | solution.py:815
  591.1 38.0 %reduce-scatter.7.cloned.1.call-done = bf16[1024,256]{1,0:T(8,128)(2,1)} async-done(((bf16[8192,256]{1,0:T(8,128)(2,1)}), bf16[1024,256]{1,0:T(8,128)(2,1)}) %reduce-scatter.7.cloned.1.call-update) | async-done | bytes 524304 | tf_op jit(solution)/shard_map/reduce_scatter | solution.py:807
  631.2 6.0 psum.28
  640.3 20.5 %all-gather.32.cloned.1.call-done = bf16[4096,256]{1,0:T(8,128)(2,1)} async-done(((bf16[1024,256]{1,0:T(8,128)(2,1)}), bf16[4096,256]{1,0:T(8,128)(2,1)}) %all-gather.32.cloned.1.call-update) | async-done | bytes 2097168 | tf_op jit(solution)/shard_map/all_gather | solution.py:837
  660.8 23.1 %attend_backward.1 = (bf16[4,1024,256]{2,1,0:T(8,128)(2,1)}, bf16[4,256,768]{2,1,0:T(8,128)(2,1)}) custom-call(bf16[4,1024,256]{2,1,0:T(8,128)(2,1)} %bitcast.68, bf16[4,256,256]{2,1,0:T(8,128)(2,1)} %slice.50.wo_ref, bf16[4,256,512]{2,1,0:T(8,128)(2,1)} %slice.46.wq_ref, bf16[1024,1024]{1,0:T(8,128)(2,1)} %get-tuple-element.30.normed_ref, ...), custom_call_target="tpu_custom_call" | custom-call | tf_op jit(solution)/shard_map/attend_backward/pallas_call | solution.py:839
  684.0 36.6 %reduce-scatter.11.cloned.1.call-done = bf16[256,768]{1,0:T(8,128)(2,1)} async-done(((bf16[1024,768]{1,0:T(8,128)(2,1)}), bf16[256,768]{1,0:T(8,128)(2,1)}) %reduce-scatter.11.cloned.1.call-update) | async-done | bytes 393232 | tf_op jit(solution)/shard_map/reduce_scatter | solution.py:863
  723.8 18.9 %collective-permute-done = bf16[256,768]{1,0:T(8,128)(2,1)S(1)} collective-permute-done((bf16[256,768]{1,0:T(8,128)(2,1)}, bf16[256,768]{1,0:T(8,128)(2,1)S(1)}, u32[]{:S(2)}, u32[]{:S(2)}) %collective-permute-start) | collective-permute-done | bytes 393248 | tf_op jit(solution)/shard_map/ppermute | solution.py:867
  749.7 17.8 %all-reduce.2.cloned.1.call-done = bf16[256,768]{1,0:T(8,128)(2,1)} async-done(((bf16[256,768]{1,0:T(8,128)(2,1)}), bf16[256,768]{1,0:T(8,128)(2,1)}) %all-reduce.2.cloned.1.call-update) | async-done | bytes 393232 | tf_op jit(solution)/shard_map/psum | solution.py:867
  773.1 27.3 %reduce-scatter.9.cloned.1.call-done = bf16[1024,256]{1,0:T(8,128)(2,1)} async-done(((bf16[4096,256]{1,0:T(8,128)(2,1)}), bf16[1024,256]{1,0:T(8,128)(2,1)}) %reduce-scatter.9.cloned.1.call-update) | async-done | bytes 524304 | tf_op jit(solution)/shard_map/reduce_scatter | solution.py:860
  802.0 7.1 psum.29
  809.9 38.0 %psum.30 = f32[34,256]{1,0:T(8,128)S(1)} all-reduce(f32[34,256]{1,0:T(8,128)S(1)} %pad_maximum_fusion.1), channel_id=1, replica_groups=mesh['dp'=2,'row'=4,'col'=4] {'dp','col'}, use_global_device_ids=true, to_apply=%region_15.16 | all-reduce | flops 8704 | bytes 69632 | tf_op jit(solution)/shard_map/psum | solution.py:881
  849.1 7.6 reduce-scatter.5.cloned.1.call-done
  (115 shorter events, 45.0 us)
Async XLA Ops:
  7.2 77.7 %copy-start.16 = (bf16[256,32]{0,1:T(8,128)(2,1)S(1)}, bf16[256,32]{0,1:T(8,128)(2,1)}, u32[]{:S(2)}) copy-start(bf16[256,32]{0,1:T(8,128)(2,1)} %param.19) | copy-start | bytes 49156
  7.2 41.3 %all-gather.22.cloned.1.call-start = ((), (), s32[]{:S(2)}) async-start(), calls=%async_computation.11 | async-start | bytes 1966080 | tf_op jit(solution)/shard_map/all_gather | solution.py:735
  10.0 83.7 %all-gather.20.cloned.1.call-start = ((), (), s32[]{:S(2)}) async-start(), calls=%async_computation.10 | async-start | bytes 2621440 | tf_op jit(solution)/shard_map/all_gather | solution.py:751
  48.6 42.9 %all-to-all-start = ((bf16[4,256,768]{2,1,0:T(8,128)(2,1)}), bf16[4,256,768]{2,1,0:T(8,128)(2,1)S(1)}, u32[]{:S(2)}, u32[]{:S(2)}) async-start(bf16[4,256,768]{2,1,0:T(8,128)(2,1)} %bitcast.65), calls=%async_computation | async-start | bytes 3145728 | tf_op jit(solution)/shard_map/all_to_all | solution.py:736
  52.6 75.3 %all-gather.24.cloned.1.call-start = ((), (), s32[]{:S(2)}) async-start(), calls=%async_computation.12 | async-start | bytes 2621440 | tf_op jit(solution)/shard_map/all_gather | solution.py:768
  107.2 78.8 %all-gather.30.cloned.1.call-start = ((), (), s32[]{:S(2)}) async-start(), calls=%async_computation.15 | async-start | bytes 1081344 | tf_op jit(solution)/shard_map/all_gather | solution.py:724
  113.0 189.7 %all-gather.28.cloned.1.call-start = ((), (), s32[]{:S(2)}) async-start(), calls=%async_computation.14 | async-start | bytes 17301504 | tf_op jit(solution)/shard_map/all_gather | solution.py:730
  113.6 305.4 %all-gather.26.cloned.1.call-start = ((), (), s32[]{:S(2)}) async-start(), calls=%async_computation.13 | async-start | bytes 17301504 | tf_op jit(solution)/shard_map/all_gather | solution.py:773
  131.6 497.4 %reduce-scatter.7.cloned.1.call-start = ((), (), s32[]{:S(2)}) async-start(), calls=%async_computation.6 | async-start | bytes 4718592 | tf_op jit(solution)/shard_map/reduce_scatter | solution.py:807
  579.1 49.9 %copy-start = (f32[1024,256]{1,0:T(8,128)S(1)}, f32[1024,256]{1,0:T(8,128)}, u32[]{:S(2)}) copy-start(f32[1024,256]{1,0:T(8,128)} %get-tuple-element.53) | copy-start | bytes 3145732
  579.1 49.9 %copy-start.17 = (bf16[256,32]{0,1:T(8,128)(2,1)S(1)}, bf16[256,32]{0,1:T(8,128)(2,1)}, u32[]{:S(2)}) copy-start(bf16[256,32]{0,1:T(8,128)(2,1)} %param.19) | copy-start | bytes 49156
  579.1 58.1 %copy-start.6 = (bf16[1024,256]{1,0:T(8,128)(2,1)S(1)}, bf16[1024,256]{1,0:T(8,128)(2,1)}, u32[]{:S(2)}) copy-start(bf16[1024,256]{1,0:T(8,128)(2,1)} %param.23) | copy-start | bytes 1572868
  579.1 81.7 %all-gather.32.cloned.1.call-start = ((), (), s32[]{:S(2)}) async-start(), calls=%async_computation.16 | async-start | bytes 2621440 | tf_op jit(solution)/shard_map/all_gather | solution.py:837
  579.2 59.1 %copy-start.19 = (f32[256]{0:T(256)}, f32[256]{0:T(256)S(1)}, u32[]{:S(2)}) copy-start(f32[256]{0:T(256)S(1)} %convert_element_type.78) | copy-start | bytes 3076
  588.6 49.7 %copy-start.8 = (f32[32,1024]{1,0:T(8,128)}, f32[32,1024]{1,0:T(8,128)S(1)}, u32[]{:S(2)}) copy-start(f32[32,1024]{1,0:T(8,128)S(1)} %reshape.142) | copy-start | bytes 393220
  638.3 82.2 %reduce-scatter.11.cloned.1.call-start = ((), (), s32[]{:S(2)}) async-start(), calls=%async_computation.8 | async-start | bytes 1966080 | tf_op jit(solution)/shard_map/reduce_scatter | solution.py:863
  683.9 60.9 %copy-start.23 = (bf16[256]{0:T(256)(128)(2,1)S(1)}, bf16[256]{0:T(256)(128)(2,1)}, u32[]{:S(2)}) copy-start(bf16[256]{0:T(256)(128)(2,1)} %param.15) | copy-start | bytes 1540
  684.0 83.6 %all-reduce.2.cloned.1.call-start = ((), (), s32[]{:S(2)}) async-start(), calls=%async_computation.9 | async-start | bytes 786432 | tf_op jit(solution)/shard_map/psum | solution.py:867
  720.6 22.2 %collective-permute-start = (bf16[256,768]{1,0:T(8,128)(2,1)}, bf16[256,768]{1,0:T(8,128)(2,1)S(1)}, u32[]{:S(2)}, u32[]{:S(2)}) collective-permute-start(bf16[256,768]{1,0:T(8,128)(2,1)} %reduce-scatter.11.cloned.1.call-done), channel_id=1, source_target_pairs={{0,0},{1,4},{2,8},{3,12},{4,1},{5,5},{6,9},{7,13},{8,2},{9,6},{10,... | collective-permute-start | bytes 1179656 | tf_op jit(solution)/shard_map/ppermute | solution.py:867
  743.5 56.9 %reduce-scatter.9.cloned.1.call-start = ((), (), s32[]{:S(2)}) async-start(), calls=%async_computation.7 | async-start | bytes 2621440 | tf_op jit(solution)/shard_map/reduce_scatter | solution.py:860
  744.3 112.4 %reduce-scatter.5.cloned.1.call-start = ((), (), s32[]{:S(2)}) async-start(), calls=%async_computation.5 | async-start | bytes 4718592 | tf_op jit(solution)/shard_map/reduce_scatter | solution.py:810
  744.3 56.1 %copy-start.2 = (bf16[1024,256]{1,0:T(8,128)(2,1)S(1)}, bf16[1024,256]{1,0:T(8,128)(2,1)}, u32[]{:S(2)}) copy-start(bf16[1024,256]{1,0:T(8,128)(2,1)} %param.14) | copy-start | bytes 1572868
  744.9 111.9 %copy-start.4 = (f32[1024,256]{1,0:T(8,128)S(1)}, f32[1024,256]{1,0:T(8,128)}, u32[]{:S(2)}) copy-start(f32[1024,256]{1,0:T(8,128)} %copy-done.3) | copy-start | bytes 3145732
  744.9 111.8 %copy-start.7 = (bf16[1024,256]{1,0:T(8,128)(2,1)S(1)}, bf16[1024,256]{1,0:T(8,128)(2,1)}, u32[]{:S(2)}) copy-start(bf16[1024,256]{1,0:T(8,128)(2,1)} %param.23) | copy-start | bytes 1572868
  (14 other events, 192.1 us)
Sparse Core Ops, SparseCore 0:
  10.2 38.3 all-gather.21
  50.1 31.6 all-gather.19
  107.3 20.5 all-gather.23
  131.3 54.7 all-gather.29
  188.8 113.8 all-gather.27
  305.9 113.0 all-gather.25
  579.3 49.7 reduce-scatter.6
  638.5 22.2 all-gather.31
  684.1 36.4 reduce-scatter.10
  743.7 23.8 all-reduce.1
  770.1 30.2 reduce-scatter.8
  804.0 52.6 reduce-scatter.4

commit v2 on v1

--- a/solution.py
+++ b/solution.py
@@ -409,6 +409,11 @@
 WINDOW = 512
 BLOCK_Q = 256
 LANES = 128
+SMALL_ROWS = 48
+GAIN_ONE = EXPERTS
+GAIN_TWO = EXPERTS + 1
+RSTD_LANE = LANES - 1
+RSTD_ROW = 8
 F32 = jnp.float32
 LOW = jnp.bfloat16
 VMEM_BYTES = 67_000_000
@@ -459,15 +464,164 @@
     return (q_at >= k_at) & (seg_col == seg_row)
 
 
+def remote(src, dst, send_sem, recv_sem, where):
+    return pltpu.make_async_remote_copy(
+        src_ref=src, dst_ref=dst, send_sem=send_sem, recv_sem=recv_sem,
+        device_id=where, device_id_type=pl.DeviceIdType.MESH,
+    )
+
+
+class Copies:
+    def __init__(self, send_sems, recv_sems):
+        self.send_sems, self.recv_sems = send_sems, recv_sems
+        self.sends = self.recvs = 0
+        self.open = []
+
+    def receivers(self, number=1):
+        first = self.recvs
+        self.recvs += number
+        return first
+
+    def send(self, src, dst, receiver, where, when=None):
+        at = self.sends
+        self.sends += 1
+        copy = remote(src, dst, self.send_sems.at[at], self.recv_sems.at[receiver], where)
+        if when is None:
+            copy.start()
+        else:
+            pl.when(when)(copy.start)
+        self.open.append((copy, when))
+
+    def local(self, src, dst, when=None):
+        at = self.sends
+        self.sends += 1
+        copy = pltpu.make_async_copy(src, dst, self.send_sems.at[at])
+        if when is None:
+            copy.start()
+        else:
+            pl.when(when)(copy.start)
+        return copy
+
+    def arrived(self, dst, receiver, where):
+        remote(dst, dst, self.recv_sems.at[receiver], self.recv_sems.at[receiver], where).wait_recv()
+
+    def finish(self):
+        for copy, when in self.open:
+            if when is None:
+                copy.wait_send()
+            else:
+                pl.when(when)(copy.wait_send)
+
+
+class Place:
+    def __init__(self, counts):
+        self.dp_count, self.row_count, self.col_count = counts
+        self.dp, self.row, self.col = (lax.axis_index(name) for name in ("dp", "row", "col"))
+        self.pair_row = self.row + 1 - 2 * lax.rem(self.row, 2)
+        self.far_row = lax.rem(self.row + 2, self.row_count)
+        self.cross_row = lax.rem(self.pair_row + 2, self.row_count)
+        self.other_dp = self.dp_count - 1 - self.dp
+        self.here = (self.dp, self.row, self.col)
+        self.pair = (self.dp, self.pair_row, self.col)
+        self.far = (self.dp, self.far_row, self.col)
+        self.over = (self.other_dp, self.row, self.col)
+        self.over_far = (self.other_dp, self.far_row, self.col)
+
+    def row_at(self, step):
+        return lax.rem(self.row + step + self.row_count, self.row_count)
+
+    def col_at(self, step):
+        return lax.rem(self.col + step + self.col_count, self.col_count)
+
+    def plane(self):
+        peers = [(self.dp, self.row_at(k), self.col) for k in range(1, self.row_count)]
+        return peers + [(self.other_dp, self.row_at(k), self.col) for k in range(self.row_count)]
+
+    def column(self):
+        return [(self.dp, self.row, self.col_at(k)) for k in range(1, self.col_count)]
+
+
+def greet(peers):
+    barrier = pltpu.get_barrier_semaphore()
+    for peer in peers:
+        pl.semaphore_signal(barrier, inc=1, device_id=peer, device_id_type=pl.DeviceIdType.MESH)
+    pl.semaphore_wait(barrier, len(peers))
+
+
 def attend_forward_kernel(
-    h_ref, gain_ref, w_ref, seg_col_ref, seg_row_ref, tab_ref,
-    mixed_ref, normed_ref, q_ref, k_ref, v_ref, lse_ref,
+    counts, hidden_hbm, own_q_hbm, own_o_hbm, small_hbm, seg_hbm, cot_hbm, tab_ref,
+    resid_ref, low_ref, mix_ref, normed_ref, q_ref, k_ref, v_ref, lse_ref, wq_ref, zo_ref, small_ref, seg_ref, cot_plane,
+    h_ref, zq_ref, own_ref, column_ref, send_sems, recv_sems,
 ):
+    place = Place(counts)
+    row_count, col_count = place.row_count, place.col_count
+    copies = Copies(send_sems, recv_sems)
     parts, length, width = h_ref.shape
     kv_heads = k_ref.shape[0]
     features = parts * width
-
-    @pl.loop(0, length // BLOCK_Q)
+    chunks = length // BLOCK_Q
+    greet(place.plane() + place.column())
+
+    h_pair, h_far, h_cross = (copies.receivers() for _ in range(3))
+    copies.send(hidden_hbm, h_ref.at[place.row], h_far, place.far)
+    copies.send(hidden_hbm, h_ref.at[place.row], h_pair, place.pair)
+    h_own = copies.local(hidden_hbm, h_ref.at[place.row])
+    zq_own = copies.local(own_q_hbm, zq_ref.at[place.col])
+    zo_own = copies.local(own_o_hbm, zo_ref.at[place.col])
+    small_own = copies.local(small_hbm, small_ref.at[place.row])
+    seg_own = copies.local(seg_hbm, seg_ref.at[place.row])
+    zq_in = copies.receivers(col_count)
+    zo_in = copies.receivers(col_count)
+    for k in range(1, col_count):
+        copies.send(own_q_hbm, zq_ref.at[place.col], zq_in + k, (place.dp, place.row, place.col_at(k)))
+    small_in, seg_in = copies.receivers(row_count), copies.receivers(row_count)
+    for k in range(1, row_count):
+        copies.send(small_hbm, small_ref.at[place.row], small_in + k, (place.dp, place.row_at(k), place.col))
+        copies.send(seg_hbm, seg_ref.at[place.row], seg_in + k, (place.dp, place.row_at(k), place.col))
+    cot_own = copies.local(cot_hbm, own_ref)
+    cot_pair, cot_in, cot_back = copies.receivers(), copies.receivers(3), copies.receivers(3)
+    own_cot = cot_plane.at[place.dp, place.row]
+    copies.send(cot_hbm, own_cot, cot_in + 1, place.over)
+    copies.send(cot_hbm, own_cot, cot_pair, place.pair)
+
+    def share_blocks(landing, result, landed, first, own):
+        waits = []
+        for k in range(col_count):
+            source = place.col_at(-k)
+            if k == 0:
+                own.wait()
+            else:
+                copies.arrived(landing.at[source], landed + k, place.here)
+            mine = source == place.row
+            step = lax.rem(source - place.row + row_count, row_count)
+            copies.send(
+                landing.at[source], result.at[place.row], first + step, (place.dp, source, place.col), source != place.row
+            )
+            waits.append((copies.local(landing.at[source], result.at[place.row], mine), mine))
+        return waits
+
+    def blocks_shared(result, first, waits):
+        for copy, mine in waits:
+            pl.when(mine)(copy.wait)
+        for k in range(1, row_count):
+            copies.arrived(result.at[place.row_at(-k)], first + k, place.here)
+
+    copies.arrived(h_ref.at[place.far_row], h_far, place.far)
+    copies.send(h_ref.at[place.far_row], h_ref.at[place.far_row], h_cross, place.pair)
+    wq_in = copies.receivers(row_count)
+    wq_waits = share_blocks(zq_ref, wq_ref, zq_in, wq_in, zq_own)
+
+    for k in range(1, col_count):
+        copies.send(own_o_hbm, zo_ref.at[place.col], zo_in + k, (place.dp, place.row, place.col_at(k)))
+    copies.send(cot_hbm, own_cot, cot_in, place.far)
+    h_own.wait()
+    copies.arrived(h_ref.at[place.pair_row], h_pair, place.pair)
+    copies.arrived(h_ref.at[place.cross_row], h_cross, place.pair)
+    small_own.wait()
+    for k in range(1, row_count):
+        copies.arrived(small_ref.at[place.row_at(-k)], small_in + k, place.here)
+
+    @pl.loop(0, chunks)
     def _(chunk):
         rows = pl.ds(pl.multiple_of(chunk * BLOCK_Q, BLOCK_Q), BLOCK_Q)
         total = jnp.zeros((BLOCK_Q, 1), F32)
@@ -475,12 +629,30 @@
             piece = h_ref[part, rows, :].astype(F32)
             total = total + jnp.sum(piece * piece, axis=1, keepdims=True)
         rstd = lax.rsqrt(total / features + EPSILON)
+        lse_ref[rows, :] = jnp.broadcast_to(rstd, (BLOCK_Q, LANES))
         for part in range(parts):
             piece = h_ref[part, rows, :].astype(F32)
-            normed_ref[rows, part * width : (part + 1) * width] = (
-                piece * rstd * gain_ref[part]
-            ).astype(LOW)
-        qkv = dot_nn(normed_ref[rows, :], w_ref[...])
+            gain = small_ref[part, GAIN_ONE : GAIN_ONE + 1, :].astype(F32)
+            normed_ref[rows, part * width : (part + 1) * width] = (piece * rstd * gain).astype(LOW)
+
+    seg_own.wait()
+    for k in range(1, row_count):
+        copies.arrived(seg_ref.at[place.row_at(-k)], seg_in + k, place.here)
+    segments = seg_ref[place.col]
+    for start in range(0, length, LANES):
+        column_ref[start : start + LANES, :] = jnp.broadcast_to(
+            segments[0:1, start : start + LANES], (LANES, LANES)
+        ).T
+
+    cot_own.wait()
+    cot_kept = copies.local(own_ref, cot_plane.at[place.dp, place.row])
+
+    blocks_shared(wq_ref, wq_in, wq_waits)
+
+    @pl.loop(0, chunks)
+    def _(chunk):
+        rows = pl.ds(pl.multiple_of(chunk * BLOCK_Q, BLOCK_Q), BLOCK_Q)
+        qkv = dot_nn(normed_ref[rows, :], wq_ref[...].reshape(features, -1))
         for head in range(kv_heads):
             base = head * 4 * HD
             queries = qkv[:, base : base + LANES]
@@ -494,12 +666,19 @@
 
     scale = HD**-0.5
     lane = lax.broadcasted_iota(jnp.int32, (BLOCK_Q, LANES), 1)
-    for block in range(length // BLOCK_Q):
+    mix_pair, mix_far, mix_cross = (copies.receivers(chunks) for _ in range(3))
+
+    def pass_on(block):
+        piece = mix_ref.at[place.far_row, pl.ds(block * BLOCK_Q, BLOCK_Q)]
+        copies.arrived(piece, mix_far + block, place.far)
+        copies.send(piece, piece, mix_cross + block, place.pair)
+
+    for block in range(chunks):
         q_start = block * BLOCK_Q
         k_start = max(0, q_start - WINDOW)
         q_rows, k_rows = slice(q_start, q_start + BLOCK_Q), slice(k_start, q_start + BLOCK_Q)
-        mask = window_mask(seg_col_ref[q_rows, :], seg_row_ref[:, k_rows], q_start, k_start)
-        logs = jnp.zeros((BLOCK_Q, LANES), F32)
+        mask = window_mask(column_ref[q_rows, 0:1], segments[0:1, k_rows], q_start, k_start)
+        logs = lse_ref[q_rows, :]
         for head in range(2 * kv_heads):
             scores = dot_nt(q_ref[head, q_rows, :], k_ref[head // 2, k_rows, :]) * scale
             scores = jnp.where(mask, scores, NEG_LARGE)
@@ -507,41 +686,139 @@
             weights = jnp.exp(scores - top)
             total = jnp.sum(weights, axis=1, keepdims=True)
             out = dot_nn(weights.astype(LOW), v_ref[head // 2, k_rows, :]) / total
-            mixed_ref[q_rows, head * HD : (head + 1) * HD] = out.astype(LOW)
+            mix_ref[place.row, q_rows, head * HD : (head + 1) * HD] = out.astype(LOW)
             logs = jnp.where(lane == head, top + jnp.log(total), logs)
         lse_ref[q_rows, :] = logs
+        piece = mix_ref.at[place.row, pl.ds(q_start, BLOCK_Q)]
+        copies.send(piece, piece, mix_far + block, place.far)
+        copies.send(piece, piece, mix_pair + block, place.pair)
+        if block > 0:
+            pass_on(block - 1)
+    pass_on(chunks - 1)
+    for k, (dp_at, row_at) in enumerate(
+        ((place.dp, place.far_row), (place.other_dp, place.row), (place.other_dp, place.far_row))
+    ):
+        piece = cot_plane.at[dp_at, row_at]
+        copies.arrived(piece, cot_in + k, place.here)
+        if k == 0:
+            copies.send(piece, piece, cot_in + 2, place.over)
+        copies.send(piece, piece, cot_back + k, place.pair)
+    zo_own.wait()
+    for k in range(1, col_count):
+        copies.arrived(zo_ref.at[place.col_at(-k)], zo_in + k, place.here)
+    for block in range(chunks):
+        rows = slice(block * BLOCK_Q, (block + 1) * BLOCK_Q)
+        window = pl.ds(block * BLOCK_Q, BLOCK_Q)
+        copies.arrived(mix_ref.at[place.pair_row, window], mix_pair + block, place.pair)
+        copies.arrived(mix_ref.at[place.cross_row, window], mix_cross + block, place.pair)
+        branch = dot_nn(mix_ref[0, rows, :], zo_ref[0])
+        for part in range(1, parts):
+            branch = branch + dot_nn(mix_ref[part, rows, :], zo_ref[part])
+        resid = h_ref[place.row, rows, :].astype(F32) + branch
+        resid_ref[rows, :] = resid
+        low_ref[rows, :] = resid.astype(LOW)
+
+    cot_kept.wait()
+    copies.arrived(cot_plane.at[place.dp, place.pair_row], cot_pair, place.pair)
+    for k, (dp_at, row_at) in enumerate(
+        ((place.dp, place.cross_row), (place.other_dp, place.pair_row), (place.other_dp, place.cross_row))
+    ):
+        copies.arrived(cot_plane.at[dp_at, row_at], cot_back + k, place.pair)
+    copies.finish()
 
 
 def attend_backward_kernel(
-    gb_ref, wo_ref, wq_ref, normed_ref, mixed_ref, q_ref, k_ref, v_ref, lse_ref, seg_col_ref, seg_row_ref, tab_ref,
-    back_ref, grads_ref,
-    gm_ref, dqkv_ref, dk_ref, dv_ref, low_ref,
+    counts, grad_low_hbm, grad_ref, hidden_ref, resid_ref, wo_ref, wq_ref, normed_ref, mix_hbm, q_ref, k_ref, v_ref, lse_ref,
+    seg_ref, small_ref, part_ref, tab_ref, y_hbm,
+    out_ref, grad_in_ref, grads_ref, sums_ref,
+    gb_ref, mixed_ref, gm_ref, dq_ref, dk_ref, dv_ref, turn_ref, column_ref, y_own_ref, y_in_ref, y_chip_ref, y_last_ref,
+    away_ref, pair_in_ref, own_ref, chip_ref, last_ref, inner_ref, parts_ref,
+    send_sems, recv_sems,
 ):
+    place = Place(counts)
+    copies = Copies(send_sems, recv_sems)
+    dp_count, row_count, col_count = counts
     parts, length, width = gb_ref.shape
     kv_heads = k_ref.shape[0]
+    features = parts * width
+    chunks = length // BLOCK_Q
     scale = HD**-0.5
+    far_side = [(place.other_dp, place.row, place.col_at(k)) for k in range(1, col_count)]
+    greet(place.plane() + place.column() + far_side)
+
+    def window(chunk):
+        return pl.ds(chunk * BLOCK_Q, BLOCK_Q)
+
+    blocks = range(chunks - 1, -1, -1)
+    gb_far, gb_pair, gb_cross = (copies.receivers(chunks) for _ in range(3))
+    for chunk in blocks:
+        piece = gb_ref.at[place.row, window(chunk)]
+        copies.send(grad_low_hbm.at[window(chunk)], piece, gb_far + chunk, place.far)
+        copies.send(grad_low_hbm.at[window(chunk)], piece, gb_pair + chunk, place.pair)
+    gb_own = copies.local(grad_low_hbm, gb_ref.at[place.row])
+    mix_own = copies.local(mix_hbm.at[place.row], mixed_ref)
+    y_pair = copies.receivers(2 * dp_count)
+    y_held = []
+    for turn, dp_at in enumerate((place.other_dp, place.dp)):
+        for q, (here, there) in enumerate(
+            ((place.row, place.pair_row), (place.far_row, place.cross_row))
+        ):
+            copies.send(y_hbm.at[dp_at, there], y_in_ref.at[turn, q], y_pair + 2 * turn + q, place.pair)
+            y_held.append(copies.local(y_hbm.at[dp_at, here], y_own_ref.at[turn, q]))
+
+    segments = seg_ref[place.col]
+    for start in range(0, length, LANES):
+        column_ref[start : start + LANES, :] = jnp.broadcast_to(
+            segments[0:1, start : start + LANES], (LANES, LANES)
+        ).T
     dk_ref[...] = jnp.zeros_like(dk_ref)
     dv_ref[...] = jnp.zeros_like(dv_ref)
-
-    @pl.loop(0, length // BLOCK_Q)
-    def _(chunk):
-        rows = pl.ds(pl.multiple_of(chunk * BLOCK_Q, BLOCK_Q), BLOCK_Q)
-        total = dot_nt(gb_ref[0, rows, :], wo_ref[0])
-        for part in range(1, parts):
-            total = total + dot_nt(gb_ref[part, rows, :], wo_ref[part])
-        for head in range(2 * kv_heads):
-            gm_ref[head, rows, :] = total[:, head * HD : (head + 1) * HD].astype(LOW)
-
-    for block in range(length // BLOCK_Q):
+    gb_own.wait()
+
+    def pass_on(chunk):
+        piece = gb_ref.at[place.far_row, window(chunk)]
+        copies.arrived(piece, gb_far + chunk, place.far)
+        copies.send(piece, piece, gb_cross + chunk, place.pair)
+
+    y_last = copies.receivers(3)
+
+    def y_sums():
+        for copy in y_held:
+            copy.wait()
+        for turn, q, slot, peer in ((0, 1, 1, place.over_far), (1, 1, 2, place.far), (0, 0, 0, place.over)):
+            copies.arrived(y_in_ref.at[turn, q], y_pair + 2 * turn + q, place.pair)
+            y_chip_ref[turn, q] = (
+                y_own_ref[turn, q].astype(F32) + y_in_ref[turn, q].astype(F32)
+            ).astype(LOW)
+            copies.send(y_chip_ref.at[turn, q], y_last_ref.at[slot], y_last + slot, peer)
+        copies.arrived(y_in_ref.at[1, 0], y_pair + 2, place.pair)
+
+    away_in = [copies.receivers(chunks) for _ in range(2)]
+    last_in = copies.receivers(chunks)
+
+    def far_share(chunk):
+        rows = slice(chunk * BLOCK_Q, (chunk + 1) * BLOCK_Q)
+        copies.arrived(pair_in_ref.at[1, window(chunk)], away_in[1] + chunk, place.pair)
+        chip_ref[rows, :] = (own_ref[1, rows, :] + pair_in_ref[1, rows, :].astype(F32)).astype(LOW)
+        copies.send(chip_ref.at[window(chunk)], last_ref.at[window(chunk)], last_in + chunk, place.far)
+
+    pass_on(chunks - 1)
+    for block in blocks:
         q_start = block * BLOCK_Q
         k_start = max(0, q_start - WINDOW)
         q_rows, k_rows = slice(q_start, q_start + BLOCK_Q), slice(k_start, q_start + BLOCK_Q)
-        mask = window_mask(seg_col_ref[q_rows, :], seg_row_ref[:, k_rows], q_start, k_start)
+        copies.arrived(gb_ref.at[place.pair_row, window(block)], gb_pair + block, place.pair)
+        copies.arrived(gb_ref.at[place.cross_row, window(block)], gb_cross + block, place.pair)
+        total = dot_nt(gb_ref[0, q_rows, :], wo_ref[0])
+        for part in range(1, parts):
+            total = total + dot_nt(gb_ref[part, q_rows, :], wo_ref[part])
+        gm_ref[...] = total.astype(LOW)
+        mask = window_mask(column_ref[q_rows, 0:1], segments[0:1, k_rows], q_start, k_start)
         logs = lse_ref[q_rows, :]
         for kv in range(kv_heads):
             keys, vals = k_ref[kv, k_rows, :], v_ref[kv, k_rows, :]
             for head in (2 * kv, 2 * kv + 1):
-                queries, grad = q_ref[head, q_rows, :], gm_ref[head, q_rows, :]
+                queries, grad = q_ref[head, q_rows, :], gm_ref[:, head * HD : (head + 1) * HD]
                 scores = dot_nt(queries, keys) * scale
                 weights = jnp.where(mask, jnp.exp(scores - logs[:, head : head + 1]), 0.0)
                 grad_weights = dot_nt(grad, vals)
@@ -549,57 +826,397 @@
                 grad_scores = (weights * (grad_weights - inner)).astype(LOW)
                 dv_ref[kv, k_rows, :] += dot_tn(weights.astype(LOW), grad)
                 dk_ref[kv, k_rows, :] += dot_tn(grad_scores, queries)
-                lanes = kv * 4 * HD + (head % 2) * HD
-                dqkv_ref[q_rows, lanes : lanes + HD] = dot_nn(grad_scores, keys) * scale
-
-    @pl.loop(0, length // BLOCK_Q)
-    def _(chunk):
-        rows = pl.ds(pl.multiple_of(chunk * BLOCK_Q, BLOCK_Q), BLOCK_Q)
+                dq_ref[:, head * HD : (head + 1) * HD] = dot_nn(grad_scores, keys) * scale
+        if block > 0:
+            pass_on(block - 1)
         for kv in range(kv_heads):
             base = kv * 4 * HD
-            queries = dqkv_ref[rows, base : base + LANES]
-            queries = queries * tab_ref[0, rows, :] - swap_halves(queries) * tab_ref[1, rows, :]
-            others = jnp.concatenate([dk_ref[kv, rows, :] * scale, dv_ref[kv, rows, :]], axis=1)
-            others = others * tab_ref[2, rows, :] - swap_halves(others) * tab_ref[3, rows, :]
-            low_ref[rows, base : base + LANES] = queries.astype(LOW)
-            low_ref[rows, base + LANES : base + 2 * LANES] = others.astype(LOW)
-        for part in range(parts):
-            back_ref[part, rows, :] = dot_nt(low_ref[rows, :], wq_ref[part]).astype(LOW)
-
-    columns = low_ref.shape[1]
+            queries = dq_ref[:, kv * LANES : (kv + 1) * LANES]
+            queries = queries * tab_ref[0, q_rows, :] - swap_halves(queries) * tab_ref[1, q_rows, :]
+            others = jnp.concatenate([dk_ref[kv, q_rows, :] * scale, dv_ref[kv, q_rows, :]], axis=1)
+            others = others * tab_ref[2, q_rows, :] - swap_halves(others) * tab_ref[3, q_rows, :]
+            turn_ref[q_rows, base : base + LANES] = queries.astype(LOW)
+            turn_ref[q_rows, base + LANES : base + 2 * LANES] = others.astype(LOW)
+        for q, row_at in ((1, place.cross_row), (0, place.pair_row)):
+            away_ref[q, q_rows, :] = dot_nt(turn_ref[q_rows, :], wq_ref[row_at]).astype(LOW)
+            copies.send(
+                away_ref.at[q, window(block)], pair_in_ref.at[q, window(block)], away_in[q] + block, place.pair
+            )
+        for q, row_at in ((1, place.far_row), (0, place.row)):
+            own_ref[q, q_rows, :] = dot_nt(turn_ref[q_rows, :], wq_ref[row_at])
+        if block == chunks - 1:
+            y_sums()
+        else:
+            far_share(block + 1)
+
+    columns = turn_ref.shape[1]
+    mix_own.wait()
     for part in range(parts):
         grads_ref[part, :, :columns] = dot_tn(
-            normed_ref[:, part * width : (part + 1) * width], low_ref[...]
+            normed_ref[:, part * width : (part + 1) * width], turn_ref[...]
         ).astype(LOW)
         grads_ref[part, :, columns:] = dot_tn(mixed_ref[...], gb_ref[part]).astype(LOW)
-
-
-def moe_kernel(
-    counts, res_hbm, cot_hbm, rk_ref, gain_ref, router_ref, wg_ref, wu_ref, wd_ref,
-    y_hbm, pb_hbm, gg_ref, gates_out_ref, logits_out_ref, dg_ref, du_ref, dd_ref,
-    res_ref, cot_ref, x_ref, gate_ref, pick_ref, eo_ref, back_ref, stage_ref, sems, out_sem,
+        if part == 0:
+            far_share(0)
+
+    gain = small_ref[place.row, GAIN_ONE : GAIN_ONE + 1, :].astype(F32)
+    inner_in = copies.receivers(row_count)
+    gain_sum = jnp.zeros((1, width), F32)
+    for chunk in blocks:
+        rows = slice(chunk * BLOCK_Q, (chunk + 1) * BLOCK_Q)
+        copies.arrived(pair_in_ref.at[0, window(chunk)], away_in[0] + chunk, place.pair)
+        copies.arrived(last_ref.at[window(chunk)], last_in + chunk, place.far)
+        grad_normed = own_ref[0, rows, :] + pair_in_ref[0, rows, :].astype(F32) + last_ref[rows, :].astype(F32)
+        own_ref[0, rows, :] = grad_normed
+        along = grad_normed * hidden_ref[rows, :].astype(F32)
+        gain_sum = gain_sum + jnp.sum(along * lse_ref[rows, RSTD_LANE : RSTD_LANE + 1], axis=0, keepdims=True)
+        inner_ref[place.row, 0:1, rows] = row_of(jnp.sum(along * gain, axis=1, keepdims=True))
+    parts_ref[0] = part_ref[...]
+    parts_ref[0, GAIN_ONE : GAIN_ONE + 1, :] = gain_sum
+    for k in range(1, row_count):
+        copies.send(
+            inner_ref.at[place.row], inner_ref.at[place.row], inner_in + k, (place.dp, place.row_at(k), place.col)
+        )
+    others = place.column() + [place.over] + far_side
+    sums_in = copies.receivers(len(others) + 1)
+    for k, peer in enumerate(others):
+        copies.send(parts_ref.at[0], parts_ref.at[k + 1], sums_in + k + 1, peer)
+
+    for slot in range(3):
+        copies.arrived(y_last_ref.at[slot], y_last + slot, place.here)
+    for chunk in range(chunks):
+        rows = slice(chunk * BLOCK_Q, (chunk + 1) * BLOCK_Q)
+        mixture = y_own_ref[1, 0, rows, :].astype(F32) + y_in_ref[1, 0, rows, :].astype(F32)
+        for slot in range(3):
+            mixture = mixture + y_last_ref[slot, rows, :].astype(F32)
+        out_ref[rows, :] = (resid_ref[rows, :] + mixture).astype(LOW)
+
+    for k in range(1, row_count):
+        copies.arrived(inner_ref.at[place.row_at(-k)], inner_in + k, place.here)
+    inner = inner_ref[0, 0:1, :]
+    for part in range(1, row_count):
+        inner = inner + inner_ref[part, 0:1, :]
+    for chunk in range(chunks):
+        rows = slice(chunk * BLOCK_Q, (chunk + 1) * BLOCK_Q)
+        rstd = lse_ref[rows, RSTD_LANE : RSTD_LANE + 1]
+        cube = rstd * rstd * rstd * column_of(inner[:, rows]) / features
+        grad_in_ref[rows, :] = (
+            grad_ref[rows, :] + rstd * (own_ref[0, rows, :] * gain) - hidden_ref[rows, :].astype(F32) * cube
+        )
+    total = parts_ref[0]
+    for k in range(len(others)):
+        copies.arrived(parts_ref.at[k + 1], sums_in + k + 1, place.here)
+        total = total + parts_ref[k + 1]
+    sums_ref[...] = total
+    copies.finish()
+
+
+def expert_grads(gate_pre, up_pre, grad_hidden):
+    sig = 1.0 / (1.0 + jnp.exp(-gate_pre))
+    silu = gate_pre * sig
+    grad_gate = grad_hidden * up_pre * (sig * (1.0 + gate_pre * (1.0 - sig)))
+    return (silu * up_pre).astype(LOW), grad_gate.astype(LOW), (grad_hidden * silu).astype(LOW)
+
+
+def slot_picks(rank_row, capacity):
+    at = lax.broadcasted_iota(jnp.int32, (capacity, rank_row.shape[1]), 0).astype(F32)
+    return at == rank_row
+
+
+def column_of(row):
+    return jnp.broadcast_to(row, (LANES, row.shape[1])).T[:, 0:1]
+
+
+def row_of(column):
+    return jnp.broadcast_to(column, (column.shape[0], LANES)).T[0:1, :]
+
+
+def experts_kernel(
+    counts, low_hbm, resid_ref, cot_own_ref, packed_hbm, cot_plane_hbm, small_ref, zo_hbm, wg_hbm, wu_hbm, wd_hbm,
+    y_hbm, grad_ref, grad_low_ref, table_ref, part_ref, wo_hbm,
+    wg_ref, wu_ref, wd_ref, res_ref, cot_ref, x_ref, packed_ref, rank_ref, gate_ref, g_ref, pick_ref, eo_ref, back_ref,
+    away_ref, pair_in_ref, own_ref, chip_ref, last_ref, stage_ref, gg_ref, gg_in_ref, rstd_ref, inner_ref, nx_ref,
+    send_sems, recv_sems,
+):
+    place = Place(counts)
+    copies = Copies(send_sems, recv_sems)
+    dp_count, row_count, col_count = counts
+    _, parts, length, width = res_ref.shape
+    experts, features, hidden_width = wg_ref.shape
+    capacity = pick_ref.shape[0] // experts
+    chunks = length // BLOCK_Q
+    total_experts = dp_count * row_count * experts
+    pair_count = length * TOP
+    first_expert = (place.dp * row_count + place.row) * experts
+    order = (place.other_dp, place.dp)
+    greet(place.plane() + place.column())
+
+    res_pair, res_far, res_over, res_across, res_cross, res_up, res_slant = (copies.receivers() for _ in range(7))
+    own_low = res_ref.at[place.dp, place.row]
+    copies.send(low_hbm, own_low, res_far, place.far)
+    copies.send(low_hbm, own_low, res_over, place.over)
+    copies.send(low_hbm, own_low, res_pair, place.pair)
+    packed_over = copies.receivers()
+    copies.send(packed_hbm, packed_ref.at[place.dp], packed_over, place.over)
+    packed_own = copies.local(packed_hbm, packed_ref.at[place.dp])
+    low_own = copies.local(low_hbm, own_low)
+    cot_in = [copies.local(cot_plane_hbm.at[dp_at], cot_ref.at[dp_at]) for dp_at in (place.dp, place.other_dp)]
+    weights_in = [copies.local(*pair) for pair in ((wg_hbm, wg_ref), (wu_hbm, wu_ref), (wd_hbm, wd_ref))]
+
+    def pass_far():
+        copies.arrived(res_ref.at[place.dp, place.far_row], res_far, place.far)
+        piece = res_ref.at[place.dp, place.far_row]
+        copies.send(piece, piece, res_across, place.over)
+        copies.send(piece, piece, res_cross, place.pair)
+
+    def pass_over():
+        piece = res_ref.at[place.other_dp, place.row]
+        copies.arrived(piece, res_over, place.over)
+        copies.send(piece, piece, res_up, place.pair)
+
+    def pass_across():
+        piece = res_ref.at[place.other_dp, place.far_row]
+        copies.arrived(piece, res_across, place.over)
+        copies.send(piece, piece, res_slant, place.pair)
+
+    def ranks_of(dp_at):
+        ids = packed_ref[dp_at] // pair_count
+        orders = (packed_ref[dp_at] - ids * pair_count).astype(F32)
+        rows = []
+        for e in range(experts):
+            match = ids == first_expert + e
+            known = jnp.max(jnp.where(match, 1.0, 0.0), axis=0, keepdims=True)
+            at = jnp.sum(jnp.where(match, orders, 0.0), axis=0, keepdims=True)
+            rows.append(jnp.where(known > 0.0, at, float(pair_count)))
+        stacked = jnp.concatenate(rows + [jnp.zeros((LANES - experts, length), F32)], axis=0)
+        columns = stacked.T
+        for e in range(experts):
+            count = jnp.zeros((1, length), F32)
+            for start in range(0, length, BLOCK_Q):
+                before = columns[start : start + BLOCK_Q, e : e + 1] < rows[e]
+                count = count + jnp.sum(jnp.where(before, 1.0, 0.0), axis=0, keepdims=True)
+            rank_ref[dp_at, e : e + 1, :] = jnp.where(rows[e] < float(pair_count), count, -1.0)
+
+    def gather_grads(dp_at):
+        @pl.loop(0, experts)
+        def _(e):
+            pick = slot_picks(rank_ref[dp_at, pl.ds(e, 1), :], capacity).astype(F32).astype(LOW)
+            slots = pl.ds(pl.multiple_of(e * capacity, capacity), capacity)
+            for part in range(parts):
+                g_ref[dp_at, part, slots, :] = dot_nn(pick, cot_ref[dp_at, part]).astype(LOW)
+
+    packed_own.wait()
+    ranks_of(place.dp)
+    pass_far()
+    cot_in[0].wait()
+    gather_grads(place.dp)
+    pass_over()
+    copies.arrived(packed_ref.at[place.other_dp], packed_over, place.over)
+    ranks_of(place.other_dp)
+    pass_across()
+    cot_in[1].wait()
+    gather_grads(place.other_dp)
+
+    wo_in = copies.receivers(row_count)
+    wo_waits = []
+    for k in range(col_count):
+        source = place.col_at(k)
+        mine = source == place.row
+        step = lax.rem(source - place.row + row_count, row_count)
+        copies.send(
+            zo_hbm.at[source], wo_hbm.at[place.row], wo_in + step, (place.dp, source, place.col), jnp.logical_not(mine)
+        )
+    own_wo = copies.local(zo_hbm.at[place.row], stage_ref.at[0, pl.ds(0, zo_hbm.shape[1])])
+
+    low_own.wait()
+    copies.arrived(res_ref.at[place.dp, place.pair_row], res_pair, place.pair)
+    copies.arrived(res_ref.at[place.dp, place.cross_row], res_cross, place.pair)
+    copies.arrived(res_ref.at[place.other_dp, place.pair_row], res_up, place.pair)
+    copies.arrived(res_ref.at[place.other_dp, place.cross_row], res_slant, place.pair)
+    for copy in weights_in:
+        copy.wait()
+    own_wo.wait()
+    kept_wo = copies.local(stage_ref.at[0, pl.ds(0, zo_hbm.shape[1])], wo_hbm.at[place.row])
+    kept_wo.wait()
+
+    own_scaled = place.row
+    gg_same, gg_other = copies.receivers(row_count), copies.receivers(row_count)
+    pair_in = copies.receivers(2 * dp_count)
+    last_over, last_across, last_far = (copies.receivers() for _ in range(3))
+    table_in = copies.receivers(col_count)
+
+    for turn, dp_at in enumerate(order):
+        last = turn == dp_count - 1
+
+        @pl.loop(0, chunks)
+        def _(chunk):
+            rows = pl.ds(pl.multiple_of(chunk * BLOCK_Q, BLOCK_Q), BLOCK_Q)
+            total = jnp.zeros((BLOCK_Q, 1), F32)
+            for part in range(parts):
+                piece = res_ref[dp_at, part, rows, :].astype(F32)
+                total = total + jnp.sum(piece * piece, axis=1, keepdims=True)
+            rstd = lax.rsqrt(total / features + EPSILON)
+            for part in range(parts):
+                piece = res_ref[dp_at, part, rows, :].astype(F32)
+                gain = small_ref[part, GAIN_TWO : GAIN_TWO + 1, :].astype(F32)
+                x_ref[rows, part * width : (part + 1) * width] = (piece * rstd * gain).astype(LOW)
+            table_ref[place.col, dp_at, RSTD_ROW : RSTD_ROW + 1, rows] = row_of(rstd)
+            if last:
+                rstd_ref[rows, :] = jnp.broadcast_to(rstd, (BLOCK_Q, LANES))
+                piece = res_ref[dp_at, own_scaled, rows, :].astype(F32)
+                gain = small_ref[own_scaled, GAIN_TWO : GAIN_TWO + 1, :].astype(F32)
+                nx_ref[rows, :] = (piece * rstd * gain).astype(LOW)
+
+        logits = jnp.zeros((total_experts, length), F32)
+        for part in range(parts):
+            logits = logits + dot_nt(
+                small_ref[part, :total_experts, :], x_ref[:, part * width : (part + 1) * width]
+            )
+        ids = packed_ref[dp_at] // pair_count
+        expert_at = lax.broadcasted_iota(jnp.int32, (total_experts, length), 0)
+        chosen = expert_at == ids[0:1, :]
+        for k in range(1, TOP):
+            chosen = chosen | (expert_at == ids[k : k + 1, :])
+        shown = jnp.where(chosen, logits, NEG_LARGE)
+        weights = jnp.where(chosen, jnp.exp(shown - jnp.max(shown, axis=0, keepdims=True)), 0.0)
+        gate_ref[...] = weights / jnp.sum(weights, axis=0, keepdims=True)
+        table_ref[place.col, dp_at, 0:experts, :] = rank_ref[dp_at, 0:experts, :]
+        for e in range(experts):
+            table_ref[place.col, dp_at, experts + e : experts + e + 1, :] = gate_ref[pl.ds(first_expert + e, 1), :]
+
+        @pl.loop(0, experts)
+        def _(e):
+            here = slot_picks(rank_ref[dp_at, pl.ds(e, 1), :], capacity)
+            pick = here.astype(F32).astype(LOW)
+            slots = pl.ds(pl.multiple_of(e * capacity, capacity), capacity)
+            pick_ref[slots, :] = pick
+            gate_slot = jnp.sum(
+                jnp.where(here, gate_ref[pl.ds(first_expert + e, 1), :], 0.0), axis=1, keepdims=True
+            )
+            x = dot_nn(pick, x_ref[...]).astype(LOW)
+            hidden, grad_gate, grad_up = None, None, None
+            grad_hidden = jnp.zeros((capacity, hidden_width), F32)
+            for part in range(parts):
+                pair_grad = (g_ref[dp_at, part, slots, :].astype(F32) * gate_slot).astype(LOW)
+                grad_hidden = grad_hidden + dot_nt(
+                    pair_grad, wd_ref[e, :, part * width : (part + 1) * width]
+                )
+            hidden, grad_gate, grad_up = expert_grads(dot_nn(x, wg_ref[e]), dot_nn(x, wu_ref[e]), grad_hidden)
+            along = jnp.zeros((capacity, 1), F32)
+            for part in range(parts):
+                cols = slice(part * width, (part + 1) * width)
+                out = dot_nn(hidden, wd_ref[e, :, cols]).astype(LOW).astype(F32)
+                along = along + jnp.sum(g_ref[dp_at, part, slots, :].astype(F32) * out, axis=1, keepdims=True)
+                eo_ref[part, slots, :] = (out * gate_slot).astype(LOW)
+                back_ref[part, slots, :] = (
+                    dot_nt(grad_gate, wg_ref[e, cols, :]) + dot_nt(grad_up, wu_ref[e, cols, :])
+                ).astype(LOW)
+            gg_ref[dp_at, pl.ds(e, 1), :] = jnp.sum(jnp.where(here, along, 0.0), axis=0, keepdims=True)
+
+        owner = place.dp * row_count + place.row
+        if last:
+            for k in range(1, row_count):
+                copies.send(gg_ref.at[dp_at], gg_in_ref.at[owner], gg_same + k, (dp_at, place.row_at(k), place.col))
+            gg_in_ref[owner] = gg_ref[dp_at]
+        else:
+            for k in range(row_count):
+                copies.send(gg_ref.at[dp_at], gg_in_ref.at[owner], gg_other + k, (dp_at, place.row_at(k), place.col))
+
+        for q, row_at in enumerate((place.pair_row, place.cross_row)):
+            away_ref[turn, q] = dot_tn(pick_ref[...], back_ref[row_at]).astype(LOW)
+            copies.send(away_ref.at[turn, q], pair_in_ref.at[turn, q], pair_in + 2 * turn + q, place.pair)
+        for q, row_at in enumerate((place.far_row, place.row)):
+            own_ref[q] = dot_tn(pick_ref[...], back_ref[row_at])
+        copies.arrived(pair_in_ref.at[turn, 1], pair_in + 2 * turn + 1, place.pair)
+        chip_ref[turn, 1] = (own_ref[0] + pair_in_ref[turn, 1].astype(F32)).astype(LOW)
+        if last:
+            copies.send(chip_ref.at[turn, 1], last_ref.at[2], last_far, place.far)
+        else:
+            copies.send(chip_ref.at[turn, 1], last_ref.at[1], last_across, place.over_far)
+        copies.arrived(pair_in_ref.at[turn, 0], pair_in + 2 * turn, place.pair)
+        if last:
+            own_ref[1] = own_ref[1] + pair_in_ref[turn, 0].astype(F32)
+        else:
+            chip_ref[turn, 0] = (own_ref[1] + pair_in_ref[turn, 0].astype(F32)).astype(LOW)
+            copies.send(chip_ref.at[turn, 0], last_ref.at[0], last_over, place.over)
+
+        for part in range(parts):
+            stage_ref[part] = dot_tn(pick_ref[...], eo_ref[part]).astype(LOW)
+        kept = copies.local(stage_ref, y_hbm.at[dp_at])
+        kept.wait()
+
+    for k in range(1, col_count):
+        copies.send(table_ref.at[place.col], table_ref.at[place.col], table_in + k, (place.dp, place.row, place.col_at(k)))
+
+    for k in range(1, row_count):
+        copies.arrived(gg_in_ref.at[place.dp * row_count + place.row_at(-k)], gg_same + k, place.here)
+    for k in range(row_count):
+        copies.arrived(gg_in_ref.at[place.other_dp * row_count + place.row_at(-k)], gg_other + k, place.here)
+    along = jnp.concatenate([gg_in_ref[owner, :experts, :] for owner in range(dp_count * row_count)], axis=0)
+    gates = gate_ref[...]
+    grad_logits = (gates * (along - jnp.sum(gates * along, axis=0, keepdims=True))).astype(LOW)
+    router = small_ref[place.row, :total_experts, :]
+    gain = small_ref[place.row, GAIN_TWO : GAIN_TWO + 1, :].astype(F32)
+    part_ref[...] = jnp.zeros_like(part_ref)
+    part_ref[:total_experts, :] = dot_nn(grad_logits, nx_ref[...])
+    own_ref[1] = own_ref[1] + dot_tn(grad_logits, router)
+
+    copies.arrived(last_ref.at[0], last_over, place.over)
+    copies.arrived(last_ref.at[1], last_across, place.over_far)
+    copies.arrived(last_ref.at[2], last_far, place.far)
+    inner_in = copies.receivers(row_count)
+    gain_sum = jnp.zeros((1, width), F32)
+    for chunk in range(chunks):
+        rows = slice(chunk * BLOCK_Q, (chunk + 1) * BLOCK_Q)
+        grad_normed = own_ref[1, rows, :]
+        for k in range(3):
+            grad_normed = grad_normed + last_ref[k, rows, :].astype(F32)
+        own_ref[0, rows, :] = grad_normed
+        along = grad_normed * resid_ref[rows, :]
+        gain_sum = gain_sum + jnp.sum(along * rstd_ref[rows, 0:1], axis=0, keepdims=True)
+        inner_ref[place.row, 0:1, rows] = row_of(jnp.sum(along * gain, axis=1, keepdims=True))
+    part_ref[GAIN_TWO : GAIN_TWO + 1, :] = gain_sum
+    for k in range(1, row_count):
+        copies.send(
+            inner_ref.at[place.row], inner_ref.at[place.row], inner_in + k, (place.dp, place.row_at(k), place.col)
+        )
+    for k in range(1, row_count):
+        copies.arrived(inner_ref.at[place.row_at(-k)], inner_in + k, place.here)
+    inner = inner_ref[0, 0:1, :]
+    for part in range(1, row_count):
+        inner = inner + inner_ref[part, 0:1, :]
+    for chunk in range(chunks):
+        rows = slice(chunk * BLOCK_Q, (chunk + 1) * BLOCK_Q)
+        rstd = rstd_ref[rows, 0:1]
+        cube = rstd * rstd * rstd * column_of(inner[:, rows]) / features
+        grad = (
+            cot_own_ref[rows, :].astype(F32) + rstd * (own_ref[0, rows, :] * gain) - resid_ref[rows, :] * cube
+        )
+        grad_ref[rows, :] = grad
+        grad_low_ref[rows, :] = grad.astype(LOW)
+
+    for k in range(1, row_count):
+        copies.arrived(wo_hbm.at[place.row_at(-k)], wo_in + k, place.here)
+    for k in range(1, col_count):
+        copies.arrived(table_ref.at[place.col_at(-k)], table_in + k, place.here)
+    copies.finish()
+
+
+def weight_grads_kernel(
+    counts, res_hbm, cot_hbm, table_ref, small_ref, wg_ref, wu_ref, wd_ref, dg_ref, du_ref, dd_ref,
+    res_ref, cot_ref, sems,
 ):
     dp_count, row_count, col_count = counts
     blocks = dp_count * col_count
-    my_dp, my_row, my_col = lax.axis_index("dp"), lax.axis_index("row"), lax.axis_index("col")
     experts, features, hidden_width = wg_ref.shape
     _, parts, length, width = res_hbm.shape
-    capacity = pick_ref.shape[0] // experts
-    first_expert = (my_dp * row_count + my_row) * experts
-
-    def block_of(step):
-        other = step - dp_count
-        far = dp_count <= step
-        dp_at = jnp.where(far, other // (col_count - 1), step)
-        col_at = jnp.where(far, lax.rem(my_col + 1 + lax.rem(other, col_count - 1), col_count), my_col)
-        return dp_at * col_count + col_at
+    capacity = length * TOP // (dp_count * row_count * experts)
 
     def fetch(step):
-        b = block_of(step)
         slot = lax.rem(step, 2)
         return (
-            pltpu.make_async_copy(res_hbm.at[b], res_ref, sems.at[0]),
-            pltpu.make_async_copy(cot_hbm.at[b], cot_ref.at[slot], sems.at[1 + slot]),
+            pltpu.make_async_copy(res_hbm.at[step], res_ref.at[slot], sems.at[slot]),
+            pltpu.make_async_copy(cot_hbm.at[step], cot_ref.at[slot], sems.at[2 + slot]),
         )
 
     for copy in fetch(0):
@@ -610,89 +1227,45 @@
 
     @pl.loop(0, blocks)
     def _(step):
-        b = block_of(step)
         slot = lax.rem(step, 2)
         for copy in fetch(step):
             copy.wait()
-
-        @pl.loop(0, length // BLOCK_Q)
-        def _(chunk):
-            rows = pl.ds(pl.multiple_of(chunk * BLOCK_Q, BLOCK_Q), BLOCK_Q)
-            total = jnp.zeros((BLOCK_Q, 1), F32)
-            for part in range(parts):
-                piece = res_ref[part, rows, :].astype(F32)
-                total = total + jnp.sum(piece * piece, axis=1, keepdims=True)
-            rstd = lax.rsqrt(total / features + EPSILON)
-            for part in range(parts):
-                piece = res_ref[part, rows, :].astype(F32)
-                x_ref[rows, part * width : (part + 1) * width] = (
-                    piece * rstd * gain_ref[part]
-                ).astype(LOW)
 
         @pl.when(step + 1 < blocks)
         def _():
             for copy in fetch(step + 1):
                 copy.start()
 
-        logits = dot_nt(router_ref[...], x_ref[...])
-        chosen = rk_ref[b] >= 0.0
-        shown = jnp.where(chosen, logits, NEG_LARGE)
-        weights = jnp.where(chosen, jnp.exp(shown - jnp.max(shown, axis=0, keepdims=True)), 0.0)
-        gates = weights / jnp.sum(weights, axis=0, keepdims=True)
-        gate_ref[...] = gates
-
-        @pl.when(step < dp_count)
-        def _():
-            gates_out_ref[step] = gates
-            logits_out_ref[step] = logits
+        dp_at, col_at = step // col_count, lax.rem(step, col_count)
 
         @pl.loop(0, experts)
         def _(e):
-            rank_row = rk_ref[b, pl.ds(first_expert + e, 1), :]
-            gate_row = gate_ref[pl.ds(first_expert + e, 1), :]
-            at = lax.broadcasted_iota(jnp.int32, (capacity, length), 0).astype(F32)
-            here = at == rank_row
+            here = slot_picks(table_ref[col_at, dp_at, pl.ds(e, 1), :], capacity)
             pick = here.astype(F32).astype(LOW)
+            gate_row = table_ref[col_at, dp_at, pl.ds(experts + e, 1), :]
             gate_slot = jnp.sum(jnp.where(here, gate_row, 0.0), axis=1, keepdims=True)
-            x = dot_nn(pick, x_ref[...]).astype(LOW)
-            g = jnp.concatenate([dot_nn(pick, cot_ref[slot, part]) for part in range(parts)], axis=1)
-            pair_grad = (g * gate_slot).astype(LOW)
-            gate_pre = dot_nn(x, wg_ref[e])
-            up_pre = dot_nn(x, wu_ref[e])
-            sig = 1.0 / (1.0 + jnp.exp(-gate_pre))
-            silu = gate_pre * sig
-            hidden = (silu * up_pre).astype(LOW)
-            grad_hidden = dot_nt(pair_grad, wd_ref[e])
-            grad_gate = (grad_hidden * up_pre * (sig * (1.0 + gate_pre * (1.0 - sig)))).astype(LOW)
-            grad_up = (grad_hidden * silu).astype(LOW)
-
-            @pl.when(step < dp_count)
-            def _():
-                slots = pl.ds(pl.multiple_of(e * capacity, capacity), capacity)
-                out = dot_nn(hidden, wd_ref[e]).astype(LOW).astype(F32)
-                along = jnp.sum(g * out, axis=1, keepdims=True)
-                gg_ref[step, pl.ds(e, 1), :] = jnp.sum(
-                    jnp.where(here, along, 0.0), axis=0, keepdims=True
-                )
-                pick_ref[slots, :] = pick
-                eo_ref[slots, :] = (out * gate_slot).astype(LOW)
-                back_ref[slots, :] = (
-                    dot_nt(grad_gate, wg_ref[e]) + dot_nt(grad_up, wu_ref[e])
-                ).astype(LOW)
-
+            rstd_row = table_ref[col_at, dp_at, RSTD_ROW : RSTD_ROW + 1, :]
+            rstd_slot = jnp.sum(jnp.where(here, rstd_row, 0.0), axis=1, keepdims=True)
+            x = jnp.concatenate(
+                [
+                    (
+                        dot_nn(pick, res_ref[slot, part])
+                        * rstd_slot
+                        * small_ref[part, GAIN_TWO : GAIN_TWO + 1, :].astype(F32)
+                    ).astype(LOW)
+                    for part in range(parts)
+                ],
+                axis=1,
+            )
+            pair_grad = jnp.concatenate(
+                [(dot_nn(pick, cot_ref[slot, part]) * gate_slot).astype(LOW) for part in range(parts)], axis=1
+            )
+            hidden, grad_gate, grad_up = expert_grads(
+                dot_nn(x, wg_ref[e]), dot_nn(x, wu_ref[e]), dot_nt(pair_grad, wd_ref[e])
+            )
             dd_ref[e] += dot_tn(hidden, pair_grad)
             dg_ref[e] += dot_tn(x, grad_gate)
             du_ref[e] += dot_tn(x, grad_up)
-
-        @pl.when(step < dp_count)
-        def _():
-            for source, target in ((back_ref, pb_hbm), (eo_ref, y_hbm)):
-                for part in range(parts):
-                    cols = slice(part * width, (part + 1) * width)
-                    stage_ref[part] = dot_tn(pick_ref[...], source[:, cols]).astype(LOW)
-                copy = pltpu.make_async_copy(stage_ref, target.at[step], out_sem)
-                copy.start()
-                copy.wait()
 
 
 def fast_device(
@@ -712,154 +1285,173 @@
     hbm = pl.BlockSpec(memory_space=pl.ANY)
     params = pltpu.CompilerParams(vmem_limit_bytes=VMEM_BYTES)
 
-    ids_t, order_t = expert_ids.T, pair_order.T
-    experts_here = EXPERTS // row_count
-    mine = my_row * experts_here + jnp.arange(experts_here, dtype=jnp.int32)
-    match = ids_t[None, :, :] == mine[:, None, None]
-    chosen = jnp.any(match, axis=1)
-    orders = jnp.sum(jnp.where(match, order_t[None], 0), axis=1)
-    orders = jnp.where(chosen, orders, length * TOP)
-    ranks = jnp.sum((orders[:, :, None] < orders[:, None, :]).astype(jnp.int32), axis=1)
-    ranks = jnp.where(chosen, jnp.minimum(ranks, capacity), -1).astype(F32)
-    rank_all = lax.all_gather(ranks, ("dp", "row", "col"), axis=0)
-    rank_all = (
-        rank_all.reshape(dp_count, row_count, col_count, experts_here, length)
-        .transpose(0, 2, 1, 3, 4)
-        .reshape(blocks, EXPERTS, length)
-    )
+    packed = (expert_ids * (length * TOP) + pair_order).T
     cot_all = lax.all_gather(cotangent, ("dp", "col", "row"), axis=0).reshape(
         blocks, row_count, length, width
     )
-
-    own = jnp.concatenate([w_qkv.reshape(width, qkv_width), w_out.reshape(head_width, width)], axis=1)
-    own_cols = lax.all_gather(own, "col", axis=0)
-    own_rows = lax.all_to_all(own_cols, "row", split_axis=0, concat_axis=0, tiled=True)
-    wq_rows = own_rows[:, :, :qkv_width]
-    wo_rows = own_rows[:, :, qkv_width:]
-    wo_cols = own_cols[:, :, qkv_width:]
-    gains = lax.all_gather(
-        jnp.concatenate([norm_gain[None], ffn_gain[None], router.T], axis=0), "row", axis=0
-    ).astype(F32)
-    gain_one, gain_two = gains[:, 0:1], gains[:, 1:2]
-    router_t = gains[:, 2:].transpose(1, 0, 2).reshape(EXPERTS, -1).astype(LOW)
-    segments = lax.dynamic_index_in_dim(
-        lax.all_gather(segment_ids, "row", axis=0), my_col, axis=0, keepdims=False
-    )
-    seg_row, seg_col = segments.reshape(1, length), segments.reshape(length, 1)
+    own_q = w_qkv.reshape(width, qkv_width)
+    own_o = w_out.reshape(head_width, width)
+    small = jnp.concatenate(
+        [router.T, norm_gain[None], ffn_gain[None], jnp.zeros((SMALL_ROWS - 2 - EXPERTS, width), LOW)], axis=0
+    )
+    seg_rows = jnp.broadcast_to(segment_ids, (8, length)).astype(F32)
     tables = jnp.asarray(rope_lanes(length))
-
-    hidden_all = lax.all_gather(hidden_in, "row", axis=0)
-    mixed, normed_one, query_rot, key_rot, value_low, logs = pl.pallas_call(
-        attend_forward_kernel,
+    counts = (dp_count, row_count, col_count)
+    (
+        resid_mid, resid_low, mixed_all, normed_one, query_rot, key_rot, value_low, logs,
+        wq_rows, wo_cols, small_all, seg_all, cot_plane,
+    ) = pl.pallas_call(
+        functools.partial(attend_forward_kernel, counts),
         out_shape=(
-            jax.ShapeDtypeStruct((length, head_width), LOW),
+            jax.ShapeDtypeStruct((length, width), F32),
+            jax.ShapeDtypeStruct((length, width), LOW),
+            jax.ShapeDtypeStruct((row_count, length, head_width), LOW),
             jax.ShapeDtypeStruct((length, D), LOW),
             jax.ShapeDtypeStruct((2 * kv_local, length, HD), LOW),
             jax.ShapeDtypeStruct((kv_local, length, HD), LOW),
             jax.ShapeDtypeStruct((kv_local, length, HD), LOW),
             jax.ShapeDtypeStruct((length, LANES), F32),
+            jax.ShapeDtypeStruct((row_count, width, qkv_width), LOW),
+            jax.ShapeDtypeStruct((col_count, head_width, width), LOW),
+            jax.ShapeDtypeStruct((row_count, SMALL_ROWS, width), LOW),
+            jax.ShapeDtypeStruct((row_count, 8, length), F32),
+            jax.ShapeDtypeStruct((dp_count, row_count, length, width), LOW),
         ),
-        in_specs=[vmem] * 6,
-        out_specs=[vmem] * 6,
-        compiler_params=params,
+        in_specs=[hbm] * 6 + [vmem],
+        out_specs=[vmem] * 12 + [hbm],
+        scratch_shapes=[
+            pltpu.VMEM((row_count, length, width), LOW),
+            pltpu.VMEM((col_count, width, qkv_width), LOW),
+            pltpu.VMEM((length, width), LOW),
+            pltpu.VMEM((length, LANES), F32),
+            pltpu.SemaphoreType.DMA((64,)),
+            pltpu.SemaphoreType.DMA((64,)),
+        ],
+        compiler_params=pltpu.CompilerParams(
+            vmem_limit_bytes=VMEM_BYTES, collective_id=1, has_side_effects=True
+        ),
+        cost_estimate=pl.CostEstimate(flops=50_000_000_000, bytes_accessed=30_000_000, transcendentals=0),
         name="attend_forward",
-    )(hidden_all, gain_one, wq_rows.reshape(D, qkv_width), seg_col, seg_row, tables)
-
-    mixed_all = lax.all_gather(mixed, "row", axis=0)
-    resid_in = hidden_in.astype(F32)
-    branch = jnp.einsum("rtc,rcd->td", mixed_all, wo_cols, preferred_element_type=F32)
-    resid_mid = resid_in + branch
-    resid_low = resid_mid.astype(LOW)
+    )(hidden_in, own_q, own_o, small, seg_rows, cotangent, tables)
     resid_all = lax.all_gather(resid_low, ("dp", "col", "row"), axis=0).reshape(
         blocks, row_count, length, width
     )
-
-    y_part, pb_part, gg_part, gates_plane, logits_plane, grad_gate, grad_up, grad_down = pl.pallas_call(
-        functools.partial(moe_kernel, (dp_count, row_count, col_count)),
+    block_low = jax.ShapeDtypeStruct((length, width), LOW)
+    block_float = jax.ShapeDtypeStruct((length, width), F32)
+    slots = exp_local * capacity
+    plane = (dp_count, row_count, length, width)
+    y_part, grad_resid, grad_low, table, small_part, wo_rows = pl.pallas_call(
+        functools.partial(experts_kernel, counts),
         out_shape=(
-            jax.ShapeDtypeStruct((dp_count, row_count, length, width), LOW),
-            jax.ShapeDtypeStruct((dp_count, row_count, length, width), LOW),
-            jax.ShapeDtypeStruct((dp_count, exp_local, length), F32),
-            jax.ShapeDtypeStruct((dp_count, EXPERTS, length), F32),
-            jax.ShapeDtypeStruct((dp_count, EXPERTS, length), F32),
+            jax.ShapeDtypeStruct(plane, LOW),
+            block_float,
+            block_low,
+            jax.ShapeDtypeStruct((col_count, dp_count, 16, length), F32),
+            jax.ShapeDtypeStruct((SMALL_ROWS, width), F32),
+            jax.ShapeDtypeStruct((row_count, head_width, width), LOW),
+        ),
+        in_specs=[hbm, vmem, vmem, hbm, hbm, vmem, hbm, hbm, hbm, hbm],
+        out_specs=[hbm] + [vmem] * 4 + [hbm],
+        scratch_shapes=[
+            pltpu.VMEM(w_gate.shape, LOW),
+            pltpu.VMEM(w_up.shape, LOW),
+            pltpu.VMEM(w_down.shape, LOW),
+            pltpu.VMEM(plane, LOW),
+            pltpu.VMEM(plane, LOW),
+            pltpu.VMEM((length, D), LOW),
+            pltpu.VMEM((dp_count, TOP, length), jnp.int32),
+            pltpu.VMEM((dp_count, 8, length), F32),
+            pltpu.VMEM((EXPERTS, length), F32),
+            pltpu.VMEM((dp_count, row_count, slots, width), LOW),
+            pltpu.VMEM((slots, length), LOW),
+            pltpu.VMEM((row_count, slots, width), LOW),
+            pltpu.VMEM((row_count, slots, width), LOW),
+            pltpu.VMEM((dp_count, 2, length, width), LOW),
+            pltpu.VMEM((dp_count, 2, length, width), LOW),
+            pltpu.VMEM((2, length, width), F32),
+            pltpu.VMEM((dp_count, 2, length, width), LOW),
+            pltpu.VMEM((3, length, width), LOW),
+            pltpu.VMEM((row_count, length, width), LOW),
+            pltpu.VMEM((dp_count, 8, length), F32),
+            pltpu.VMEM((dp_count * row_count, 8, length), F32),
+            pltpu.VMEM((length, LANES), F32),
+            pltpu.VMEM((row_count, 8, length), F32),
+            pltpu.VMEM((length, width), LOW),
+            pltpu.SemaphoreType.DMA((80,)),
+            pltpu.SemaphoreType.DMA((80,)),
+        ],
+        compiler_params=pltpu.CompilerParams(
+            vmem_limit_bytes=VMEM_BYTES, collective_id=2, has_side_effects=True
+        ),
+        cost_estimate=pl.CostEstimate(flops=80_000_000_000, bytes_accessed=50_000_000, transcendentals=0),
+        name="experts",
+    )(resid_low, resid_mid, cotangent, packed, cot_plane, small_all, wo_cols, w_gate, w_up, w_down)
+
+    halves = (dp_count, 2, length, width)
+    half = (2, length, width)
+    layer_out, grad_in, grads_part, small = pl.pallas_call(
+        functools.partial(attend_backward_kernel, counts),
+        out_shape=(
+            block_low,
+            block_float,
+            jax.ShapeDtypeStruct((row_count, width, qkv_width + width), LOW),
+            jax.ShapeDtypeStruct((SMALL_ROWS, width), F32),
+        ),
+        in_specs=[hbm] + [vmem] * 6 + [hbm] + [vmem] * 8 + [hbm],
+        out_specs=[vmem] * 4,
+        scratch_shapes=[
+            pltpu.VMEM((row_count, length, width), LOW),
+            pltpu.VMEM((length, head_width), LOW),
+            pltpu.VMEM((BLOCK_Q, head_width), LOW),
+            pltpu.VMEM((BLOCK_Q, head_width), F32),
+            pltpu.VMEM((kv_local, length, HD), F32),
+            pltpu.VMEM((kv_local, length, HD), F32),
+            pltpu.VMEM((length, qkv_width), LOW),
+            pltpu.VMEM((length, LANES), F32),
+            pltpu.VMEM(halves, LOW),
+            pltpu.VMEM(halves, LOW),
+            pltpu.VMEM(halves, LOW),
+            pltpu.VMEM((3, length, width), LOW),
+            pltpu.VMEM(half, LOW),
+            pltpu.VMEM(half, LOW),
+            pltpu.VMEM(half, F32),
+            pltpu.VMEM((length, width), LOW),
+            pltpu.VMEM((length, width), LOW),
+            pltpu.VMEM((row_count, 8, length), F32),
+            pltpu.VMEM((dp_count * col_count, SMALL_ROWS, width), F32),
+            pltpu.SemaphoreType.DMA((80,)),
+            pltpu.SemaphoreType.DMA((80,)),
+        ],
+        compiler_params=pltpu.CompilerParams(
+            vmem_limit_bytes=VMEM_BYTES, collective_id=3, has_side_effects=True
+        ),
+        cost_estimate=pl.CostEstimate(flops=40_000_000_000, bytes_accessed=30_000_000, transcendentals=0),
+        name="attend_backward",
+    )(
+        grad_low, grad_resid, hidden_in, resid_mid, wo_rows, wq_rows, normed_one, mixed_all, query_rot, key_rot,
+        value_low, logs, seg_all, small_all, small_part, tables, y_part,
+    )
+
+    (grads_part, cot_all, resid_all) = lax.optimization_barrier((grads_part, cot_all, resid_all))
+    grad_gate, grad_up, grad_down = pl.pallas_call(
+        functools.partial(weight_grads_kernel, counts),
+        out_shape=(
             jax.ShapeDtypeStruct(w_gate.shape, F32),
             jax.ShapeDtypeStruct(w_up.shape, F32),
             jax.ShapeDtypeStruct(w_down.shape, F32),
         ),
-        in_specs=[hbm, hbm] + [vmem] * 6,
-        out_specs=[hbm, hbm] + [vmem] * 6,
+        in_specs=[hbm, hbm] + [vmem] * 5,
+        out_specs=[vmem] * 3,
         scratch_shapes=[
-            pltpu.VMEM((row_count, length, width), LOW),
             pltpu.VMEM((2, row_count, length, width), LOW),
-            pltpu.VMEM((length, D), LOW),
-            pltpu.VMEM((EXPERTS, length), F32),
-            pltpu.VMEM((exp_local * capacity, length), LOW),
-            pltpu.VMEM((exp_local * capacity, D), LOW),
-            pltpu.VMEM((exp_local * capacity, D), LOW),
-            pltpu.VMEM((row_count, length, width), LOW),
-            pltpu.SemaphoreType.DMA((3,)),
-            pltpu.SemaphoreType.DMA,
+            pltpu.VMEM((2, row_count, length, width), LOW),
+            pltpu.SemaphoreType.DMA((4,)),
         ],
         compiler_params=params,
-        name="experts",
-    )(resid_all, cot_all, rank_all, gain_two, router_t, w_gate, w_up, w_down)
-
-    grad_expert = lax.psum_scatter(
-        pb_part.reshape(-1, width), ("dp", "row"), scatter_dimension=0, tiled=True
-    ).astype(F32)
-    mixture = lax.psum_scatter(
-        y_part.reshape(-1, width), ("dp", "row"), scatter_dimension=0, tiled=True
-    ).astype(F32)
-    layer_out = (resid_mid + mixture).astype(LOW)
-
-    gg_all = lax.all_gather(gg_part, ("dp", "row"), axis=0)
-    gg = lax.dynamic_index_in_dim(gg_all, my_dp, axis=1, keepdims=False).reshape(EXPERTS, length)
-    gates = lax.dynamic_index_in_dim(gates_plane, my_dp, axis=0, keepdims=False)
-    inner_gate = jnp.sum(gates * gg, axis=0, keepdims=True)
-    grad_logits = gates * (gg - inner_gate)
-
-    gain_float = ffn_gain.astype(F32)
-    router_float = router.astype(F32)
-    block_all = lax.dynamic_index_in_dim(
-        resid_all, my_dp * col_count + my_col, axis=0, keepdims=False
-    ).astype(F32)
-    rstd_two = lax.rsqrt(jnp.sum(block_all * block_all, axis=(0, 2)) / D + EPSILON)[:, None]
-    grad_top = cotangent.astype(F32)
-    grad_normed = grad_expert + jnp.einsum("et,de->td", grad_logits, router_float)
-    normed_float = resid_mid * rstd_two * gain_float
-    grad_router = jnp.einsum("td,et->de", normed_float, grad_logits)
-    grad_gain_two = jnp.sum(grad_normed * resid_mid * rstd_two, axis=0)
-    scaled_two = grad_normed * gain_float
-    inner_two = lax.psum(jnp.sum(scaled_two * resid_mid, axis=1), "row")[:, None]
-    grad_resid = (
-        grad_top + rstd_two * scaled_two - resid_mid * (rstd_two * rstd_two * rstd_two * inner_two / D)
-    )
-    branch_all = lax.all_gather(grad_resid.astype(LOW), "row", axis=0)
-
-    back_part, grads_part = pl.pallas_call(
-        attend_backward_kernel,
-        out_shape=(
-            jax.ShapeDtypeStruct((row_count, length, width), LOW),
-            jax.ShapeDtypeStruct((row_count, width, qkv_width + width), LOW),
-        ),
-        in_specs=[vmem] * 12,
-        out_specs=[vmem] * 2,
-        scratch_shapes=[
-            pltpu.VMEM((2 * kv_local, length, HD), LOW),
-            pltpu.VMEM((length, qkv_width), F32),
-            pltpu.VMEM((kv_local, length, HD), F32),
-            pltpu.VMEM((kv_local, length, HD), F32),
-            pltpu.VMEM((length, qkv_width), LOW),
-        ],
-        compiler_params=params,
-        name="attend_backward",
-    )(
-        branch_all, wo_rows, wq_rows, normed_one, mixed, query_rot, key_rot, value_low, logs,
-        seg_col, seg_row, tables,
-    )
-    grad_normed_one = lax.psum_scatter(
-        back_part.reshape(-1, width), "row", scatter_dimension=0, tiled=True
-    ).astype(F32)
+        cost_estimate=pl.CostEstimate(flops=86_000_000_000, bytes_accessed=70_000_000, transcendentals=0),
+        name="weight_grads",
+    )(resid_all, cot_all, table, small_all, w_gate, w_up, w_down)
+
     grads_own = lax.psum_scatter(
         grads_part.reshape(row_count * width, -1), "col", scatter_dimension=0, tiled=True
     )
@@ -867,25 +1459,13 @@
     grads_own = lax.psum(lax.ppermute(grads_own, ("row", "col"), swap), "dp").astype(F32)
     grad_qkv = grads_own[:, :qkv_width].reshape(w_qkv.shape)
     grad_out = grads_own[:, qkv_width:].reshape(w_out.shape)
-
-    gain_first = norm_gain.astype(F32)
-    hid_float = hidden_all.astype(F32)
-    rstd_one = lax.rsqrt(jnp.sum(hid_float * hid_float, axis=(0, 2)) / D + EPSILON)[:, None]
-    grad_gain_one = jnp.sum(grad_normed_one * resid_in * rstd_one, axis=0)
-    scaled_one = grad_normed_one * gain_first
-    inner_one = lax.psum(jnp.sum(scaled_one * resid_in, axis=1), "row")[:, None]
-    grad_in = (
-        grad_resid + rstd_one * scaled_one - resid_in * (rstd_one * rstd_one * rstd_one * inner_one / D)
-    )
-    small = jnp.concatenate([grad_router.T, grad_gain_one[None], grad_gain_two[None]], axis=0)
-    small = lax.psum(small, ("dp", "col"))
     return (
         layer_out,
         grad_in,
-        small[EXPERTS],
+        small[GAIN_ONE],
         grad_qkv,
         grad_out,
-        small[EXPERTS + 1],
+        small[GAIN_TWO],
         small[:EXPERTS].T,
         grad_gate,
         grad_up,

time: 876 us -> 546 us (0.62)
  waiting for transfers between devices: 505 us -> 52.5 us
  Pallas kernels: 197 us -> 451 us
  blocking collectives: 95.7 us -> 0 us
  other arithmetic: 19.5 us -> 3.47 us
    pallas_call x3 -> x4, Pallas kernels: 197 us -> 451 us  [the longest x1 136 us: fast_device(): pl.pallas_call(functools.partial(experts_kernel, counts), out_shape=(jax....]
    all_gather x5 -> x0, waiting for transfers between devices: 126 us -> none  [the longest x1 53.5 us: fast_device(): rank_all = lax.all_gather(ranks, ('dp', 'row', 'col'), axis=0)]
    all_gather x1, waiting for transfers between devices: 116 us -> 0.02 us  [fast_device(): lax.all_gather(resid_low, ('dp', 'col', 'row'), axis=0)]
    all_gather x1, waiting for transfers between devices: 114 us -> 0.02 us  [fast_device(): lax.all_gather(cotangent, ('dp', 'col', 'row'), axis=0)]
    reduce_scatter x3 -> x0, waiting for transfers between devices: 72.8 us -> none  [the longest x1 38 us: fast_device(): lax.psum_scatter(pb_part.reshape(-1, width), ('dp', 'row'), scatter_dimen...]
    psum x3 -> x0, blocking collectives: 51.1 us -> none  [the longest x1 38 us: fast_device(): small = lax.psum(small, ('dp', 'col'))]
    all_gather x3 -> x0, blocking collectives: 44.6 us -> none  [the longest x1 30.6 us: fast_device(): lax.all_gather(segment_ids, 'row', axis=0)]
    psum x1, waiting for transfers between devices: 17.8 us -> 0.02 us  [fast_device(): lax.psum(lax.ppermute(grads_own, ('row', 'col'), swap), 'dp').astype(F32)]
  transfers between devices with their start and end apart: 14 -> 5, of which waited for: 12 -> 2; matrix products, arithmetic and copies ran while one was open for 4% -> 2% of each run, Pallas kernels for 0% -> 84%
where the time goes in v2:
time: 546 us; the launch traced here: 539 us
  Pallas kernels  451 us (83%)
  waiting for transfers between devices  52.5 us (10%)
  between operations  14.3 us (3%)
  local copies, waits for them, and re-layouts  13.8 us (3%)
    pallas_call x1, Pallas kernels, fast_device(): pl.pallas_call(functools.partial(experts_kernel, counts), out_shape=(jax....  136 us
    pallas_call x1, Pallas kernels, fast_device(): pl.pallas_call(functools.partial(weight_grads_kernel, counts), out_shape=...  114 us
    pallas_call x1, Pallas kernels, fast_device(): pl.pallas_call(functools.partial(attend_backward_kernel, counts), out_sha...  109 us
    pallas_call x1, Pallas kernels, fast_device(): pl.pallas_call(functools.partial(attend_forward_kernel, counts), out_shap...  92.3 us
    reduce_scatter x1, waiting for transfers between devices, fast_device(): lax.psum_scatter(grads_part.reshape(row_count * width, -1), 'col', scatte...  35.5 us
    ppermute x1, waiting for transfers between devices, fast_device(): lax.ppermute(grads_own, ('row', 'col'), swap)  16.2 us
  transfers between devices with their start and end apart: 5, of which 2 were waited for; matrix products, arithmetic and copies ran while one was open for 2% of the time, Pallas kernels for 84%

profile of v2, /device:TPU:2, one launch (start us, length us, event | category | flops | bytes accessed | tf_op | source)
XLA Modules:
  0.0 538.8 jit_solution(4934538177336653307)
XLA Ops:
  7.2 0.7 all-gather.5.cloned.1.call-update
  8.0 0.7 broadcast_in_dim.14
  8.6 0.7 broadcast_in_dim.15
  9.3 0.7 convert_element_type.8
  10.0 1.7 copy.24
  11.7 1.4 maximum_maximum_fusion.small_hbm
  13.1 0.6 broadcast_in_dim.17.seg_hbm
  13.8 92.3 %attend_forward.1 = (f32[1024,256]{1,0:T(8,128)}, bf16[1024,256]{1,0:T(8,128)(2,1)}, bf16[4,1024,256]{2,1,0:T(8,128)(2,1)}, bf16[1024,1024]{1,0:T(8,128)(2,1)}, ...) custom-call(bf16[1024,256]{1,0:T(8,128)(2,1)} %hidden_ref.1, ...), custom_call_target="tpu_custom_call" | custom-call | flops 49999998976 | bytes 30000000 | tf_op jit(solution)/shard_map/attend_forward/pallas_call | solution.py:1303
  106.1 0.3 reduce-scatter.2.cloned.1.call-start
  106.4 1.4 add_bitcast_fusion.packed_hbm
  107.7 136.0 %experts.1 = (bf16[2,4,1024,256]{3,2,1,0:T(8,128)(2,1)}, f32[1024,256]{1,0:T(8,128)}, bf16[1024,256]{1,0:T(8,128)(2,1)}, f32[4,2,16,1024]{3,2,1,0:T(8,128)}, f32...) custom-call(bf16[1024,256]{1,0:T(8,128)(2,1)} %get-tuple-element.39.low_hbm, f32[1024,256]{1,0:T(8,128)} %get-tuple-element.40.resid_ref, ...), custom_call_target="tpu_custom_call" | custom-call | flops 80000000000 | bytes 50000000 | tf_op jit(solution)/shard_map/experts/pallas_call | solution.py:1343
  243.7 108.6 %attend_backward.1 = (bf16[1024,256]{1,0:T(8,128)(2,1)}, f32[1024,256]{1,0:T(8,128)}, bf16[4,256,768]{2,1,0:T(8,128)(2,1)}, f32[48,256]{1,0:T(8,128)}) custom-call(bf16[1024,256]{1,0:T(8,128)(2,1)} %get-tuple-element.44.grad_low_hbm, f32[1024,256]{1,0:T(8,128)} %get-tuple-element.45.grad_ref, bf16[1024,256]{1,0:T(8,128)(2,1)} %hidden_ref.1, ...), custom_call_target="tpu_custom_call" | custom-call | flops 40000000000 | bytes 30000000 | tf_op jit(solution)/shard_map/attend_backward/pallas_call | solution.py:1392
  352.5 35.5 %reduce-scatter.2.cloned.1.call-done = bf16[256,768]{1,0:T(8,128)(2,1)} async-done(((bf16[1024,768]{1,0:T(8,128)(2,1)}), bf16[256,768]{1,0:T(8,128)(2,1)}) %reduce-scatter.2.cloned.1.call-update) | async-done | bytes 393232 | tf_op jit(solution)/shard_map/reduce_scatter | solution.py:1455
  387.9 3.3 collective-permute-start
  391.2 1.3 fusion
  392.6 1.4 slice_bitcast_fusion
  393.9 16.2 %collective-permute-done = bf16[256,768]{1,0:T(8,128)(2,1)S(1)} collective-permute-done((bf16[256,768]{1,0:T(8,128)(2,1)}, bf16[256,768]{1,0:T(8,128)(2,1)S(1)}, u32[]{:S(2)}, u32[]{:S(2)}) %collective-permute-start) | collective-permute-done | bytes 393248 | tf_op jit(solution)/shard_map/ppermute | solution.py:1459
  410.1 0.7 copy-done.1
  410.9 114.1 %weight_grads.1 = (f32[4,1024,512]{2,1,0:T(8,128)}, f32[4,1024,512]{2,1,0:T(8,128)}, f32[4,512,1024]{2,1,0:T(8,128)}) custom-call(bf16[8,4,1024,256]{3,2,1,0:T(8,128)(2,1)} %bitcast.24, bf16[8,4,1024,256]{3,2,1,0:T(8,128)(2,1)} %bitcast.23, f32[4,2,16,1024]{3,2,1,0:T(8,128)} %get-tuple-element.64.table_ref, bf16[4,48,256]{2,1,0:T(8,128)(2,1)} %get-tuple-element.42.small_ref, ...), custom_call_target="tpu_custom_call" | custom-call | flops 86000001024 | bytes 70000000 | tf_op jit(solution)/shard_map/weight_grads/pallas_call | solution.py:1436
  525.1 1.1 slice.20
  526.2 1.1 reshape.47
  527.3 1.6 slice.21
  528.9 1.9 copy.28
  530.8 1.0 copy.29
  (16 shorter events, 0.3 us)
Async XLA Ops:
  7.2 345.2 %all-gather.5.cloned.1.call-start = ((), (), s32[]{:S(2)}) async-start(), calls=%async_computation.3 | async-start | bytes 17301504 | tf_op jit(solution)/shard_map/all_gather | solution.py:1289
  7.9 344.5 %all-gather.7.cloned.1.call-start = ((), (), s32[]{:S(2)}) async-start(), calls=%async_computation.4 | async-start | bytes 17301504 | tf_op jit(solution)/shard_map/all_gather | solution.py:1336
  13.7 92.6 %copy-start.2 = (s32[1024,8]{0,1:T(8,128)S(1)}, s32[1024,8]{0,1:T(8,128)}, u32[]{:S(2)}) copy-start(s32[1024,8]{0,1:T(8,128)} %param.26) | copy-start | bytes 98308
  106.1 281.8 %reduce-scatter.2.cloned.1.call-start = ((), (), s32[]{:S(2)}) async-start(), calls=%async_computation.1 | async-start | bytes 1966080 | tf_op jit(solution)/shard_map/reduce_scatter | solution.py:1455
  352.4 172.7 %all-reduce.2.cloned.1.call-start = ((), (), s32[]{:S(2)}) async-start(), calls=%async_computation.2 | async-start | bytes 786432 | tf_op jit(solution)/shard_map/psum | solution.py:1459
  387.9 22.2 %collective-permute-start = (bf16[256,768]{1,0:T(8,128)(2,1)}, bf16[256,768]{1,0:T(8,128)(2,1)S(1)}, u32[]{:S(2)}, u32[]{:S(2)}) collective-permute-start(bf16[256,768]{1,0:T(8,128)(2,1)} %reduce-scatter.2.cloned.1.call-done), channel_id=1, source_target_pairs={{0,0},{1,4},{2,8},{3,12},{4,1},{5,5},{6,9},{7,13},{8,2},{9,6},{10,... | collective-permute-start | bytes 1179656 | tf_op jit(solution)/shard_map/ppermute | solution.py:1459
  410.1 0.7 copy-start.1
  525.1 5.7 %copy-start = (f32[1024,256]{1,0:T(8,128)S(1)}, f32[1024,256]{1,0:T(8,128)}, u32[]{:S(2)}) copy-start(f32[1024,256]{1,0:T(8,128)} %get-tuple-element.81) | copy-start | bytes 3145732
Sparse Core Ops, SparseCore 0:
  10.8 152.6 all-gather.4
  166.4 184.5 all-gather.6
  353.3 34.5 reduce-scatter.1
  411.0 23.8 all-reduce.1
